TPU v7x, 128 devices: a whole 4x4x4 slice. The times are simulated.
128 devices in a mesh: seq: 16 (over y, z), tp: 8 (over x, core).
Axes of the slice: x: 4, y: 4, z: 4, core: 2. Of those that a mesh axis runs over, the one named last changes fastest.
Arguments:
- stream_in: bfloat16 [2048, 2880], P('seq'), may hold values from -40 to 40
- attn_gain: float32 [2880], replicated, may hold values from 0.1 to 1.9
- w_qkv: bfloat16 [2880, 8, 640], P(None, 'tp'), may hold values from -2 to 2
- key_value_cache: bfloat16 [128, 8, 128], P(None, 'tp'), may hold values from -6 to 6
- w_out: bfloat16 [4096, 2880], P('tp'), may hold values from -0.09375 to 0.09375
- mlp_gain: float32 [2880], replicated, may hold values from 0.1 to 1.9
- expert_index: int32 [2048, 4], P(('seq', 'tp')), may hold values from 0 to 31, all different within a row; in each aligned block of 16 rows (0 to 15, 16 to 31, ...) at most 4 rows name the same one
- gate_weight: float32 [2048, 4], P(('seq', 'tp')), may hold values from 0.05 to 0.5
- w_gateup: bfloat16 [32, 2880, 2, 2880], P('seq', None, None, 'tp'), may hold values from -0.109375 to 0.109375
- w_down: bfloat16 [32, 2880, 2880], P('seq', 'tp'), may hold values from -0.109375 to 0.109375
Outputs:
- stream_out: bfloat16 [2048, 2880], P(('seq', 'tp'))
Inputs may be any that keep to these rules, and one draw needn't show every extreme that they name: `expert_index`: in the rows of one device (aligned blocks of 16 rows) no expert is named by more than 4 rows, a bound that some block reaches; a row names 4 different experts.
All inputs are finite; a program needn't handle non-finite values.
Results may differ from a plain program's by a relative error of at most 0.01.
Values may be sent and summed in bfloat16 or wider, within the bound.
A program may use at most 128 MiB of HBM per device.

v0:
```python
import jax
import jax.numpy as jnp
from jax import lax
from jax.sharding import PartitionSpec as P

MODEL_WIDTH = 2880
QUERY_HEADS = 64
KEY_VALUE_HEADS = 8
HEAD_SIZE = 64
WINDOW_KEYS = 128
EXPERTS = 32
TOPK = 4


EPS = 1e-05


def from_behind(value, axis, steps):
    count = lax.axis_size(axis)
    first, last = (max(0, -steps), min(count, count - steps))
    return lax.ppermute(value, axis, [(source, source + steps) for source in range(first, last)])


def rms_scale(values, gain_vec):
    mean_sq = jnp.mean(values * values, axis=-1, keepdims=True)
    return values * lax.rsqrt(mean_sq + EPS) * gain_vec


def window_block(queries, key_rows, value_rows):
    scores = jnp.einsum(
        "qhgc,khc->hgqk", queries, key_rows, preferred_element_type=jnp.float32
    ) * HEAD_SIZE ** (-0.5)
    key_offset = jnp.arange(key_rows.shape[0])[None, :] - jnp.arange(queries.shape[0])[:, None]
    in_window = (key_offset >= 1) & (key_offset <= WINDOW_KEYS)
    scores = jnp.where(in_window, scores, -1e30)
    row_max = jnp.max(scores, axis=-1, keepdims=True)
    exponent = jnp.exp(scores - row_max)
    layer_weights = (exponent / jnp.sum(exponent, axis=-1, keepdims=True)).astype(jnp.bfloat16)
    attended = jnp.einsum(
        "hgqk,khc->qhgc", layer_weights, value_rows, preferred_element_type=jnp.float32
    )
    return attended.astype(jnp.bfloat16)


def local(
    stream_in,
    attn_gain,
    w_qkv,
    key_value_cache,
    w_out,
    mlp_gain,
    expert_index,
    gate_weight,
    w_gateup,
    w_down,
):
    seq_count = lax.axis_size("seq")
    tp_count = lax.axis_size("tp")
    length_local = stream_in.shape[0]
    heads_local = w_qkv.shape[1]
    query_group_width = QUERY_HEADS // KEY_VALUE_HEADS
    normed = rms_scale(stream_in.astype(jnp.float32), attn_gain).astype(jnp.bfloat16)
    projected_rows = jnp.einsum(
        "td,dhc->thc", normed, w_qkv, preferred_element_type=jnp.float32
    ).astype(jnp.bfloat16)
    projected_rows = projected_rows.reshape(
        length_local, heads_local, query_group_width + 2, HEAD_SIZE
    )
    queries = projected_rows[:, :, :query_group_width]
    kv_tail_rows = jnp.concatenate(
        [
            projected_rows[length_local - WINDOW_KEYS :, :, query_group_width],
            projected_rows[length_local - WINDOW_KEYS :, :, query_group_width + 1],
        ],
        axis=-1,
    )
    earlier = from_behind(kv_tail_rows, "seq", 1)
    at_start = lax.axis_index("seq") == 0
    earlier = jnp.where(at_start, key_value_cache, earlier)
    key_rows = jnp.concatenate(
        [earlier[:, :, :HEAD_SIZE], projected_rows[:, :, query_group_width]], axis=0
    )
    value_rows = jnp.concatenate(
        [earlier[:, :, HEAD_SIZE:], projected_rows[:, :, query_group_width + 1]], axis=0
    )
    attended = window_block(queries, key_rows, value_rows).reshape(
        length_local, heads_local * query_group_width * HEAD_SIZE
    )
    block_rows = length_local // tp_count
    attn_out = lax.psum_scatter(
        jnp.dot(attended, w_out, preferred_element_type=jnp.float32).astype(jnp.bfloat16),
        "tp",
        scatter_dimension=0,
        tiled=True,
    ).astype(jnp.float32)
    own_start = lax.axis_index("tp") * block_rows
    residual = (
        lax.dynamic_slice_in_dim(stream_in, own_start, block_rows, 0).astype(jnp.float32) + attn_out
    )
    hidden_in = rms_scale(residual, mlp_gain).astype(jnp.bfloat16)
    experts_dev = w_gateup.shape[0]
    capacity = 2 * length_local * TOPK // (tp_count * EXPERTS)
    slots_dev = experts_dev * capacity
    onehot = (
        expert_index.reshape(-1)[:, None] == jnp.arange(EXPERTS, dtype=jnp.int32)[None, :]
    ).astype(jnp.int32)
    slot_rank = jnp.sum((jnp.cumsum(onehot, axis=0) - 1) * onehot, axis=1)
    slot_id = (expert_index.reshape(-1) * capacity + slot_rank).reshape(block_rows, TOPK)
    slot_grid = jnp.arange(EXPERTS * capacity, dtype=jnp.int32)
    matches = slot_grid[None, None, :] == slot_id[:, :, None]
    placer = jnp.sum(matches.astype(jnp.float32), axis=1).T.astype(jnp.bfloat16)
    packed = jnp.dot(placer, hidden_in, preferred_element_type=jnp.float32).astype(jnp.bfloat16)
    packed = packed.reshape(seq_count, slots_dev, MODEL_WIDTH)
    copies = jnp.broadcast_to(packed[:, None], (seq_count, tp_count, slots_dev, MODEL_WIDTH))
    copies = copies.reshape(seq_count * tp_count, slots_dev, MODEL_WIDTH)
    gathered = lax.all_to_all(copies, ("seq", "tp"), split_axis=0, concat_axis=0, tiled=True)
    gathered = gathered.reshape(seq_count, tp_count, experts_dev, capacity, MODEL_WIDTH)

    def one_expert(chosen, gate_up_matrix, down_proj):
        input_rows = chosen.reshape(-1, MODEL_WIDTH)
        gate_up_rows = jnp.einsum(
            "vi,ipk->vpk", input_rows, gate_up_matrix, preferred_element_type=jnp.float32
        )
        activated = (jax.nn.silu(gate_up_rows[:, 0]) * gate_up_rows[:, 1]).astype(jnp.bfloat16)
        result = jnp.dot(activated, down_proj, preferred_element_type=jnp.float32)
        return result.reshape(seq_count, tp_count, capacity, MODEL_WIDTH)

    partials = jnp.stack(
        [
            one_expert(gathered[:, :, expert], w_gateup[expert], w_down[expert])
            for expert in range(experts_dev)
        ],
        axis=2,
    )
    rounded = partials.astype(jnp.bfloat16).reshape(seq_count * tp_count, slots_dev, MODEL_WIDTH)
    returned = lax.all_to_all(rounded, ("seq", "tp"), split_axis=0, concat_axis=0, tiled=True)
    returned = returned.reshape(seq_count, tp_count, slots_dev, MODEL_WIDTH)
    returned_rows = jnp.sum(returned.astype(jnp.float32), axis=1).astype(jnp.bfloat16)
    returned_rows = returned_rows.reshape(EXPERTS * capacity, MODEL_WIDTH)
    picker = jnp.sum(gate_weight[:, :, None] * matches.astype(jnp.float32), axis=1)
    mixture = jnp.dot(picker, returned_rows.astype(jnp.float32), precision=lax.Precision.HIGHEST)
    return (residual + mixture).astype(jnp.bfloat16)


def solution(mesh):
    in_specs = (
        P("seq", None),
        P(),
        P(None, "tp", None),
        P(None, "tp", None),
        P("tp", None),
        P(),
        P(("seq", "tp"), None),
        P(("seq", "tp"), None),
        P("seq", None, None, "tp"),
        P("seq", "tp", None),
    )
    out_specs = P(("seq", "tp"), None)
    return jax.shard_map(local, mesh=mesh, in_specs=in_specs, out_specs=out_specs, check_vma=False)
```

profile of v0, /device:TPU:1, one launch (start us, length us, event | category | flops | bytes accessed | tf_op | source)
XLA Modules:
  0.0 269.4 jit_solution(8113619228664187838)
XLA Ops:
  6.5 1.7 fusion.17
  8.2 3.8 %fusion.22 = bf16[128,640]{1,0:T(8,128)(2,1)S(1)} fusion(bf16[2880,1,640]{2,0,1:T(8,128)(2,1)} %param.12, bf16[128,2880]{0,1:T(8,128)(2,1)} %param.10, f32[2880]{0:T(1024)} %param.11, f32[128]{0:T(128)S(1)} %add_rsqrt_fusion.1), kind=kOutput, calls=%fused_computation.32 | convolution fusion | flops 473415680 | bytes 4599552 | tf_op jit(solution)/shard_map/td,dhc->thc/dot_general | solution.py:63
  12.2 4.4 %collective-permute-start = (bf16[128,1,128]{0,2,1:T(8,128)(2,1)S(1)}, bf16[128,1,128]{0,2,1:T(8,128)(2,1)S(1)}, u32[]{:S(2)}, u32[]{:S(2)}) collective-permute-start(bf16[128,1,128]{0,2,1:T(8,128)(2,1)S(1)} %pad_maximum_fusion.1), channel_id=1, source_target_pairs={{0,8},{8,16},{16,24},{24,32},{32,40},{40,48},{48,56},{56,64},{64,7... | collective-permute-start | bytes 98312 | tf_op jit(solution)/shard_map/ppermute | solution.py:21
  16.7 0.8 collective-permute-done
  18.4 2.0 convolution_convert_fusion.3
  21.2 1.4 constant_dynamic-slice_fusion
  22.9 29.9 %reduce-scatter.2.cloned.1.call-done = bf16[16,2880]{1,0:T(8,128)(2,1)} async-done(((bf16[128,2880]{1,0:T(8,128)(2,1)}), bf16[16,2880]{1,0:T(8,128)(2,1)}) %reduce-scatter.2.cloned.1.call-update) | async-done | bytes 92176 | tf_op jit(solution)/shard_map/reduce_scatter | solution.py:90
  52.8 1.0 multiply_reduce_fusion
  53.8 1.4 convolution_convert_fusion.2
  55.2 0.3 copy.109
  55.6 0.4 broadcast_in_dim.15
  56.0 82.4 %all_to_all.10 = bf16[128,8,2880]{2,1,0:T(8,128)(2,1)S(1)} all-to-all(bf16[128,8,2880]{2,1,0:T(8,128)(2,1)S(1)} %bitcast.91), channel_id=1, replica_groups=mesh['seq'=16,'tp'=8] {'seq','tp'}, dimensions={0} | all-to-all | bytes 11796480 | tf_op jit(solution)/shard_map/all_to_all | solution.py:116
  138.4 1.0 copy.110
  139.4 0.5 fusion.48
  139.9 3.9 %copy.111 = bf16[16,8,1,4,2880]{4,3,1,0,2:T(4,128)(2,1)} copy(bf16[16,8,1,4,2880]{4,1,0,3,2:T(8,128)(2,1)S(1)} %get-tuple-element.7) | data formatting | bytes 5898240 | tf_op jit(solution)/shard_map/slice | solution.py:130
  143.8 5.6 %reshape_squeeze.6 = bf16[512,2880]{1,0:T(8,128)(2,1)} reshape(bf16[16,8,1,4,2880]{4,3,1,0,2:T(4,128)(2,1)} %copy.111) | data formatting | bytes 5898240 | tf_op jit(solution)/shard_map/reshape;squeeze | solution.py:120
  149.4 5.6 %fusion.2 = f32[512,2,360]{0,2,1:T(8,128)S(1)} fusion(bf16[2,2880,2,360]{1,3,2,0:T(8,128)(2,1)} %param.18, bf16[512,2880]{1,0:T(8,128)(2,1)} %reshape_squeeze.6), kind=kOutput, calls=%fused_computation.6 | convolution fusion | flops 2123366400 | bytes 8728576 | tf_op jit(solution)/shard_map/vi,ipk->vpk/dot_general | solution.py:121
  155.1 0.9 fusion.29
  156.0 1.2 copy.113
  157.2 0.9 reshape.111
  158.1 3.9 %copy.115 = bf16[16,8,1,4,2880]{4,3,1,0,2:T(4,128)(2,1)} copy(bf16[16,8,1,4,2880]{4,1,0,3,2:T(8,128)(2,1)S(1)} %get-tuple-element.8) | data formatting | bytes 5898240 | tf_op jit(solution)/shard_map/slice | solution.py:130
  162.0 4.6 %reshape_squeeze.7 = bf16[512,2880]{1,0:T(8,128)(2,1)S(1)} reshape(bf16[16,8,1,4,2880]{4,3,1,0,2:T(4,128)(2,1)} %copy.115) | data formatting | bytes 5898240 | tf_op jit(solution)/shard_map/reshape;squeeze | solution.py:120
  166.6 4.7 %fusion = f32[512,2,360]{0,2,1:T(8,128)S(1)} fusion(bf16[2,2880,2,360]{1,3,2,0:T(8,128)(2,1)} %param.18, bf16[512,2880]{1,0:T(8,128)(2,1)S(1)} %reshape_squeeze.7), kind=kOutput, calls=%fused_computation.4 | convolution fusion | flops 2123366400 | bytes 8663040 | tf_op jit(solution)/shard_map/vi,ipk->vpk/dot_general | solution.py:121
  171.9 0.4 copy-done.3
  172.3 3.3 %fusion.6 = bf16[16,8,1,4,2880]{4,1,3,0,2:T(8,128)(2,1)S(1)} fusion(bf16[2,360,2880]{2,1,0:T(8,128)(2,1)} %param.19, bf16[16,8,4,360]{3,2,1,0:T(4,128)(2,1)S(1)} %copy-done.3), kind=kOutput, calls=%fused_computation.10 | convolution fusion | flops 1063157760 | bytes 5437440 | tf_op jit(solution)/shard_map/dot_general | solution.py:125
  175.7 3.3 %fusion.7 = bf16[16,8,1,4,2880]{4,1,3,0,2:T(8,128)(2,1)S(1)} fusion(bf16[2,360,2880]{2,1,0:T(8,128)(2,1)} %param.19, bf16[16,8,4,360]{3,2,1,0:T(4,128)(2,1)S(1)} %reshape.112), kind=kOutput, calls=%fused_computation.11 | convolution fusion | flops 1063157760 | bytes 5437440 | tf_op jit(solution)/shard_map/dot_general | solution.py:125
  179.0 0.6 pad_maximum_fusion
  179.7 0.8 copy.119
  180.5 3.3 %copy.120 = bf16[128,8,2880]{2,1,0:T(8,128)(2,1)S(1)} copy(bf16[128,8,2880]{2,0,1:T(8,128)(2,1)S(1)} %bitcast.92) | data formatting | bytes 11796480 | tf_op jit(solution)/shard_map/convert_element_type | solution.py:135
  183.8 76.8 %all_to_all.11 = bf16[128,8,2880]{2,1,0:T(8,128)(2,1)S(1)} all-to-all(bf16[128,8,2880]{2,1,0:T(8,128)(2,1)S(1)} %copy.120), channel_id=1, replica_groups=mesh['seq'=16,'tp'=8] {'seq','tp'}, dimensions={0} | all-to-all | bytes 11796480 | tf_op jit(solution)/shard_map/all_to_all | solution.py:136
  260.6 0.8 bitcast_reduce_fusion
  261.5 1.1 fusion.10
  (42 shorter events, 2.9 us)
Async XLA Ops:
  6.5 11.9 %copy-start = (bf16[512,2880]{0,1:T(8,128)(2,1)S(1)}, bf16[512,2880]{0,1:T(8,128)(2,1)}, u32[]{:S(2)}) copy-start(bf16[512,2880]{0,1:T(8,128)(2,1)} %param.14) | copy-start | bytes 8847364
  6.5 10.1 %copy-start.4 = (bf16[128,1,128]{2,0,1:T(8,128)(2,1)S(1)}, bf16[128,1,128]{2,0,1:T(8,128)(2,1)}, u32[]{:S(2)}) copy-start(bf16[128,1,128]{2,0,1:T(8,128)(2,1)} %param.13) | copy-start | bytes 98308
  6.5 46.3 %reduce-scatter.2.cloned.1.call-start = ((), (), s32[]{:S(2)}) async-start(), calls=%async_computation.3 | async-start | bytes 847872 | tf_op jit(solution)/shard_map/reduce_scatter | solution.py:90
  12.2 5.4 %collective-permute-start = (bf16[128,1,128]{0,2,1:T(8,128)(2,1)S(1)}, bf16[128,1,128]{0,2,1:T(8,128)(2,1)S(1)}, u32[]{:S(2)}, u32[]{:S(2)}) collective-permute-start(bf16[128,1,128]{0,2,1:T(8,128)(2,1)S(1)} %pad_maximum_fusion.1), channel_id=1, source_target_pairs={{0,8},{8,16},{16,24},{24,32},{32,40},{40,48},{48,56},{56,64},{64,7... | collective-permute-start | bytes 98312 | tf_op jit(solution)/shard_map/ppermute | solution.py:21
  18.4 2.1 copy-start.6
  18.4 4.4 %copy-start.7 = (f32[16,4]{0,1:T(4,128)S(1)}, f32[16,4]{0,1:T(4,128)}, u32[]{:S(2)}) copy-start(f32[16,4]{0,1:T(4,128)} %param.17) | copy-start | bytes 772
  18.4 35.4 %copy-start.5 = (f32[2880]{0:T(1024)S(1)}, f32[2880]{0:T(1024)}, u32[]{:S(2)}) copy-start(f32[2880]{0:T(1024)} %param.15) | copy-start | bytes 34564
  171.3 1.0 copy-start.3
  183.8 78.8 %copy-start.1 = (bf16[512,2880]{0,1:T(8,128)(2,1)S(1)}, bf16[512,2880]{0,1:T(8,128)(2,1)}, u32[]{:S(2)}) copy-start(bf16[512,2880]{0,1:T(8,128)(2,1)} %param.14) | copy-start | bytes 8847364
  260.6 0.9 copy-start.2
Sparse Core Ops, SparseCore 0:
  20.6 32.1 reduce-scatter.1
where the time goes:
time: 270 us; the launch traced here: 269 us
  blocking collectives  159 us (59%)
  waiting for transfers between devices  30.7 us (11%)
  local copies, waits for them, and re-layouts  29.6 us (11%)
  matrix products  25.8 us (10%)
  between operations  13.7 us (5%)
  other arithmetic  5.97 us (2%)
  starting transfers between devices  4.37 us (2%)
    all_to_all x1, blocking collectives, local(): lax.all_to_all(copies, ('seq', 'tp'), split_axis=0, concat_axis=0, tiled=...  82.4 us
    all_to_all x1, blocking collectives, local(): lax.all_to_all(rounded, ('seq', 'tp'), split_axis=0, concat_axis=0, tiled...  76.8 us
    reduce_scatter x1, waiting for transfers between devices, local(): lax.psum_scatter(jnp.dot(attended, w_out, preferred_element_type=jnp.floa...  29.9 us
    dot_general x2, matrix products, one_expert(): jnp.einsum('vi,ipk->vpk', input_rows, gate_up_matrix, preferred_element_t...  10.3 us
    another operation x2, local copies, waits for them, and re-layouts, one_expert(): input_rows = chosen.reshape(-1, MODEL_WIDTH)  10.2 us
    slice x3, local copies, waits for them, and re-layouts, local(): gathered[:, :, expert]  8.36 us
    dot_general x2, matrix products, one_expert(): result = jnp.dot(activated, down_proj, preferred_element_type=jnp.float32)  6.68 us
  transfers between devices with their start and end apart: 2, of which 2 were waited for; matrix products, arithmetic and copies ran while one was open for 1% of the time, Pallas kernels for 0%

commit v1 on v0

v1 whole, which is shorter than its diff:
```python
import functools

import jax
import jax.numpy as jnp
from jax import lax
from jax.experimental import pallas as pl
from jax.experimental.pallas import tpu as pltpu
from jax.sharding import PartitionSpec as P

MODEL_WIDTH = 2880
QUERY_HEADS = 64
KEY_VALUE_HEADS = 8
HEAD_SIZE = 64
WINDOW_KEYS = 128
EXPERTS = 32
TOPK = 4


EPS = 1e-05


def from_behind(value, axis, steps):
    count = lax.axis_size(axis)
    first, last = (max(0, -steps), min(count, count - steps))
    return lax.ppermute(value, axis, [(source, source + steps) for source in range(first, last)])


def rms_scale(values, gain_vec):
    mean_sq = jnp.mean(values * values, axis=-1, keepdims=True)
    return values * lax.rsqrt(mean_sq + EPS) * gain_vec


def window_block(queries, key_rows, value_rows):
    scores = jnp.einsum(
        "qhgc,khc->hgqk", queries, key_rows, preferred_element_type=jnp.float32
    ) * HEAD_SIZE ** (-0.5)
    key_offset = jnp.arange(key_rows.shape[0])[None, :] - jnp.arange(queries.shape[0])[:, None]
    in_window = (key_offset >= 1) & (key_offset <= WINDOW_KEYS)
    scores = jnp.where(in_window, scores, -1e30)
    row_max = jnp.max(scores, axis=-1, keepdims=True)
    exponent = jnp.exp(scores - row_max)
    layer_weights = (exponent / jnp.sum(exponent, axis=-1, keepdims=True)).astype(jnp.bfloat16)
    attended = jnp.einsum(
        "hgqk,khc->qhgc", layer_weights, value_rows, preferred_element_type=jnp.float32
    )
    return attended.astype(jnp.bfloat16)


class Copies:
    def __init__(self, send_sems):
        self.send_sems = send_sems
        self.started = []

    def start(self, src, dst, recv_sem, seq, tp):
        copy = pltpu.make_async_remote_copy(
            src_ref=src,
            dst_ref=dst,
            send_sem=self.send_sems.at[len(self.started)],
            recv_sem=recv_sem,
            device_id=(seq, tp),
            device_id_type=pl.DeviceIdType.MESH,
        )
        copy.start()
        self.started.append(copy)

    def drain(self):
        for copy in self.started:
            copy.wait_send()


def arrived(ref, sem):
    pltpu.make_async_copy(ref, ref, sem).wait()


def moe_kernel(
    n_seq,
    n_x,
    part,
    stream_rows,
    gain,
    placer,
    picker,
    w_gateup_hbm,
    w_down_hbm,
    out,
    attn_pair,
    attn_sum,
    attn_in,
    residual,
    hidden,
    packed,
    rows,
    w_gateup,
    w_down,
    product,
    from_pair,
    chip_sum,
    ring_opp,
    ring_in,
    final,
    returned,
    mixed,
    mixed_in,
    load_sems,
    send_sems,
    attn_sems,
    block_sems,
    ring_sems,
    pair_sems,
    back_sems,
):
    seq, tp = lax.axis_index("seq"), lax.axis_index("tp")
    x, core = tp // 2, tp % 2
    nz = 4 if n_seq % 4 == 0 else n_seq
    ny = n_seq // nz
    y, z = seq // nz, seq % nz
    partner = tp + 1 - 2 * core
    right_x, left_x, far_x = (x + 1) % n_x, (x + n_x - 1) % n_x, (x + 2) % n_x
    right, left, far = right_x * 2 + core, left_x * 2 + core, far_x * 2 + core
    chunk = max(1, n_seq // 4)
    chunks = n_seq // chunk
    half = chunks // 2
    half_rows = n_seq // 2
    width = out.shape[-1]
    copies = Copies(send_sems)

    loads = [
        pltpu.make_async_copy(w_gateup_hbm, w_gateup, load_sems.at[0]),
        pltpu.make_async_copy(w_down_hbm, w_down, load_sems.at[1]),
    ]
    for load in loads:
        load.start()

    def behind(slot):
        dy, dz = slot // nz, slot % nz
        return ((y + ny - dy) % ny) * nz + (z + nz - dz) % nz

    def ahead(slot):
        dy, dz = slot // nz, slot % nz
        return ((y + dy) % ny) * nz + (z + dz) % nz

    barrier = pltpu.get_barrier_semaphore()
    for slot in range(1, n_seq):
        pl.semaphore_signal(
            barrier, inc=1, device_id=(ahead(slot), tp), device_id_type=pl.DeviceIdType.MESH
        )
    for peer in (partner, right, left, far):
        pl.semaphore_signal(
            barrier, inc=1, device_id=(seq, peer), device_id_type=pl.DeviceIdType.MESH
        )
    pl.semaphore_wait(barrier, n_seq - 1 + 4)

    copies.start(part.at[1 - core], attn_pair, attn_sems.at[0], seq, partner)
    arrived(attn_pair, attn_sems.at[0])
    attn_sum[...] = (
        part[core].astype(jnp.float32) + attn_pair[...].astype(jnp.float32)
    ).astype(jnp.bfloat16)
    for step, peer_x in ((1, far_x), (0, right_x), (2, left_x)):
        copies.start(
            attn_sum.at[peer_x], attn_in.at[step], attn_sems.at[1 + step], seq, peer_x * 2 + core
        )
    total = stream_rows[...].astype(jnp.float32) + attn_sum[x].astype(jnp.float32)
    for step in range(3):
        arrived(attn_in.at[step], attn_sems.at[1 + step])
    for step in range(3):
        total = total + attn_in[step].astype(jnp.float32)
    residual[...] = total
    hidden[core] = rms_scale(total, gain[...]).astype(jnp.bfloat16)
    copies.start(hidden.at[core], hidden.at[core], attn_sems.at[4], seq, partner)
    arrived(hidden.at[1 - core], attn_sems.at[4])

    both = hidden[...].reshape(-1, width)
    packed[...] = (
        jnp.dot(placer[...], both, preferred_element_type=jnp.float32)
        .reshape(packed.shape)
        .astype(jnp.bfloat16)
    )
    for group in range(chunks):
        for slot in range(group * chunk, (group + 1) * chunk):
            if slot:
                copies.start(
                    packed.at[behind(slot)],
                    rows.at[core, x, slot],
                    block_sems.at[group],
                    behind(slot),
                    tp,
                )
    rows[core, x, 0] = packed[seq]

    def slots(group):
        return pl.ds(group * chunk, chunk)

    for group in range(chunks):
        first = 1 if group == 0 else 0
        if chunk > first:
            got = rows.at[core, x, pl.ds(group * chunk + first, chunk - first)]
            arrived(got, block_sems.at[group])
        own = rows.at[core, x, slots(group)]
        copies.start(own, own, ring_sems.at[0, group], seq, right)
        copies.start(own, own, ring_sems.at[1, group], seq, left)
        copies.start(own, own, pair_sems.at[0, group], seq, partner)

    for load in loads:
        load.wait()

    def compute(block_x):
        def one(expert, carry):
            taken = rows[expert, block_x].reshape(n_seq * 8, width)
            contract = (((1,), (1,)), ((), ()))
            gate = lax.dot_general(
                taken, w_gateup[expert, 0], contract, preferred_element_type=jnp.float32
            )
            up = lax.dot_general(
                taken, w_gateup[expert, 1], contract, preferred_element_type=jnp.float32
            )
            activated = (gate / (1.0 + jnp.exp(-gate)) * up).astype(jnp.bfloat16)
            result = jnp.dot(activated, w_down[expert], preferred_element_type=jnp.float32)
            product[expert, block_x] = result.reshape(n_seq, 8, width).astype(jnp.bfloat16)
            return carry

        lax.fori_loop(0, 2, one, 0)

    def to_pair(block_x, which):
        copies.start(
            product.at[1 - core, block_x],
            from_pair.at[block_x],
            back_sems.at[which],
            seq,
            partner,
        )

    def pair_sum(block_x, which):
        arrived(from_pair.at[block_x], back_sems.at[which])
        chip_sum[block_x] = (
            product[core, block_x].astype(jnp.float32) + from_pair[block_x].astype(jnp.float32)
        ).astype(jnp.bfloat16)

    for group in range(chunks):
        arrived(rows.at[1 - core, x, slots(group)], pair_sems.at[0, group])
    compute(x)
    to_pair(x, 0)

    for group in range(chunks):
        got = rows.at[core, left_x, slots(group)]
        arrived(got, ring_sems.at[0, group])
        if group < half:
            copies.start(got, got, ring_sems.at[2, group], seq, right)
        copies.start(got, got, pair_sems.at[1, group], seq, partner)
        got = rows.at[core, right_x, slots(group)]
        arrived(got, ring_sems.at[1, group])
        if group >= half:
            copies.start(got, got, ring_sems.at[2, group], seq, left)
        copies.start(got, got, pair_sems.at[2, group], seq, partner)
    for group in range(chunks):
        arrived(rows.at[1 - core, left_x, slots(group)], pair_sems.at[1, group])
    compute(left_x)
    to_pair(left_x, 1)
    for group in range(chunks):
        arrived(rows.at[1 - core, right_x, slots(group)], pair_sems.at[2, group])
    compute(right_x)
    to_pair(right_x, 2)

    low, high = pl.ds(0, half_rows), pl.ds(half_rows, half_rows)
    pair_sum(left_x, 1)
    copies.start(chip_sum.at[left_x, low], ring_in.at[1, low], back_sems.at[4], seq, left)
    pair_sum(right_x, 2)
    copies.start(chip_sum.at[right_x, high], ring_in.at[0, high], back_sems.at[5], seq, right)

    for group in range(chunks):
        got = rows.at[core, far_x, slots(group)]
        arrived(got, ring_sems.at[2, group])
        copies.start(got, got, pair_sems.at[3, group], seq, partner)
    for group in range(chunks):
        arrived(rows.at[1 - core, far_x, slots(group)], pair_sems.at[3, group])
    compute(far_x)
    to_pair(far_x, 3)
    pair_sum(far_x, 3)
    copies.start(chip_sum.at[far_x, low], ring_opp.at[0], back_sems.at[6], seq, right)
    copies.start(chip_sum.at[far_x, high], ring_opp.at[1], back_sems.at[7], seq, left)
    pair_sum(x, 0)

    arrived(ring_opp.at[0], back_sems.at[6])
    chip_sum[right_x, low] = (
        chip_sum[right_x, low].astype(jnp.float32) + ring_opp[0].astype(jnp.float32)
    ).astype(jnp.bfloat16)
    copies.start(chip_sum.at[right_x, low], ring_in.at[0, low], back_sems.at[8], seq, right)
    arrived(ring_opp.at[1], back_sems.at[7])
    chip_sum[left_x, high] = (
        chip_sum[left_x, high].astype(jnp.float32) + ring_opp[1].astype(jnp.float32)
    ).astype(jnp.bfloat16)
    copies.start(chip_sum.at[left_x, high], ring_in.at[1, high], back_sems.at[9], seq, left)

    for part_rows, at, sems in ((low, 0, (8, 4)), (high, half_rows, (5, 9))):
        arrived(ring_in.at[0, part_rows], back_sems.at[sems[0]])
        arrived(ring_in.at[1, part_rows], back_sems.at[sems[1]])
        final[part_rows] = (
            chip_sum[x, part_rows].astype(jnp.float32)
            + ring_in[0, part_rows].astype(jnp.float32)
            + ring_in[1, part_rows].astype(jnp.float32)
        ).astype(jnp.bfloat16)
        for slot in range(at, at + half_rows):
            if slot:
                copies.start(
                    final.at[slot], returned.at[seq], back_sems.at[10 + slot], ahead(slot), tp
                )
    returned[seq] = final[0]
    for slot in range(1, n_seq):
        arrived(returned.at[behind(slot)], back_sems.at[10 + slot])
    terms = jnp.dot(
        picker[...],
        returned[...].reshape(n_seq * 8, width),
        preferred_element_type=jnp.float32,
    )
    count = mixed.shape[1]
    mixture = terms[: 2 * count] + terms[2 * count : 4 * count] + terms[4 * count :]
    mixed[...] = mixture.reshape(mixed.shape)
    copies.start(mixed.at[1 - core], mixed_in, attn_sems.at[5], seq, partner)
    arrived(mixed_in, attn_sems.at[5])
    out[...] = (residual[...] + (mixed[core] + mixed_in[...])).astype(jnp.bfloat16)
    copies.drain()


def moe(part, stream_rows, gain, placer, picker, w_gateup, w_down):
    n_seq = lax.axis_size("seq")
    n_x = lax.axis_size("tp") // 2
    count, width = stream_rows.shape
    hidden = w_down.shape[1]
    bf16, f32 = jnp.bfloat16, jnp.float32
    vmem, dma = pltpu.VMEM, pltpu.SemaphoreType.DMA
    chunks = n_seq // max(1, n_seq // 4)
    scratch = [
        vmem((n_x, count, width), bf16),
        vmem((n_x, count, width), bf16),
        vmem((3, count, width), bf16),
        vmem((count, width), f32),
        vmem((2, count, width), bf16),
        vmem((n_seq, 8, width), bf16),
        vmem((2, n_x, n_seq, 8, width), bf16),
        vmem((2, 2, hidden, width), bf16),
        vmem((2, hidden, width), bf16),
        vmem((2, n_x, n_seq, 8, width), bf16),
        vmem((n_x, n_seq, 8, width), bf16),
        vmem((n_x, n_seq, 8, width), bf16),
        vmem((2, n_seq // 2, 8, width), bf16),
        vmem((2, n_seq, 8, width), bf16),
        vmem((n_seq, 8, width), bf16),
        vmem((n_seq, 8, width), bf16),
        vmem((2, count, width), f32),
        vmem((count, width), f32),
        dma((2,)),
        dma((128,)),
        dma((6,)),
        dma((chunks,)),
        dma((3, chunks)),
        dma((4, chunks)),
        dma((10 + n_seq,)),
    ]
    in_vmem = pl.BlockSpec(memory_space=pltpu.VMEM)
    return pl.pallas_call(
        functools.partial(moe_kernel, n_seq, n_x),
        out_shape=jax.ShapeDtypeStruct((count, width), bf16),
        in_specs=[in_vmem] * 5 + [pl.BlockSpec(memory_space=pl.ANY)] * 2,
        out_specs=in_vmem,
        scratch_shapes=scratch,
        compiler_params=pltpu.CompilerParams(
            collective_id=0, has_side_effects=True, vmem_limit_bytes=60 * 1024 * 1024
        ),
    )(part, stream_rows, gain, placer, picker, w_gateup, w_down)


def routing(expert_index, gate_weight, seq_count, core):
    count = expert_index.shape[0]
    experts = 2 * seq_count
    own = jnp.concatenate([expert_index.astype(jnp.float32), gate_weight], axis=1)
    tp_count = lax.axis_size("tp")
    other = lax.ppermute(own, "tp", [(i, i ^ 1) for i in range(tp_count)])
    both = jnp.where(core == 0, jnp.stack([own, other]), jnp.stack([other, own]))
    holder = jnp.arange(seq_count, dtype=jnp.int32)
    named = both[:, :, :TOPK].astype(jnp.int32)[..., None] == (2 * holder + core)
    chosen = jnp.sum(named.astype(jnp.float32), axis=2)
    weight = jnp.sum(jnp.where(named, both[:, :, TOPK:, None], 0.0), axis=2)
    rank = jnp.cumsum(chosen, axis=1) - chosen
    place = jnp.arange(4, dtype=jnp.float32)
    hit = chosen[..., None] * (rank[..., None] == place)
    eye = jnp.eye(2, dtype=jnp.float32)
    hit = hit[:, :, :, None, :] * eye[:, None, None, :, None]
    picker = hit * weight[..., None, None]
    shape = (2 * count, seq_count * 8)
    placer = hit.reshape(shape).T.astype(jnp.bfloat16)
    picker = picker.reshape(shape)
    high = picker.astype(jnp.bfloat16)
    rest = picker - high.astype(jnp.float32)
    middle = rest.astype(jnp.bfloat16)
    low = (rest - middle.astype(jnp.float32)).astype(jnp.bfloat16)
    return placer, jnp.concatenate([high, middle, low], axis=0)


def local(
    stream_in,
    attn_gain,
    w_qkv,
    key_value_cache,
    w_out,
    mlp_gain,
    expert_index,
    gate_weight,
    w_gateup,
    w_down,
):
    seq_count = lax.axis_size("seq")
    tp_count = lax.axis_size("tp")
    tp = lax.axis_index("tp")
    length_local = stream_in.shape[0]
    heads_local = w_qkv.shape[1]
    query_group_width = QUERY_HEADS // KEY_VALUE_HEADS
    placer, picker = routing(expert_index, gate_weight, seq_count, tp % 2)
    normed = rms_scale(stream_in.astype(jnp.float32), attn_gain).astype(jnp.bfloat16)
    projected_rows = jnp.einsum(
        "td,dhc->thc", normed, w_qkv, preferred_element_type=jnp.float32
    ).astype(jnp.bfloat16)
    projected_rows = projected_rows.reshape(
        length_local, heads_local, query_group_width + 2, HEAD_SIZE
    )
    queries = projected_rows[:, :, :query_group_width]
    kv_tail_rows = jnp.concatenate(
        [
            projected_rows[length_local - WINDOW_KEYS :, :, query_group_width],
            projected_rows[length_local - WINDOW_KEYS :, :, query_group_width + 1],
        ],
        axis=-1,
    )
    earlier = from_behind(kv_tail_rows, "seq", 1)
    at_start = lax.axis_index("seq") == 0
    earlier = jnp.where(at_start, key_value_cache, earlier)
    key_rows = jnp.concatenate(
        [earlier[:, :, :HEAD_SIZE], projected_rows[:, :, query_group_width]], axis=0
    )
    value_rows = jnp.concatenate(
        [earlier[:, :, HEAD_SIZE:], projected_rows[:, :, query_group_width + 1]], axis=0
    )
    attended = window_block(queries, key_rows, value_rows).reshape(
        length_local, heads_local * query_group_width * HEAD_SIZE
    )
    block_rows = length_local // tp_count
    part = jnp.dot(attended, w_out, preferred_element_type=jnp.float32).astype(jnp.bfloat16)
    part = part.reshape(tp_count // 2, 2, block_rows, MODEL_WIDTH).transpose(1, 0, 2, 3)
    stream_rows = lax.dynamic_slice_in_dim(stream_in, tp * block_rows, block_rows, 0)
    return moe(
        part,
        stream_rows,
        mlp_gain[None],
        placer,
        picker,
        w_gateup.transpose(0, 2, 3, 1),
        w_down,
    )


def solution(mesh):
    in_specs = (
        P("seq", None),
        P(),
        P(None, "tp", None),
        P(None, "tp", None),
        P("tp", None),
        P(),
        P(("seq", "tp"), None),
        P(("seq", "tp"), None),
        P("seq", None, None, "tp"),
        P("seq", "tp", None),
    )
    out_specs = P(("seq", "tp"), None)
    return jax.shard_map(local, mesh=mesh, in_specs=in_specs, out_specs=out_specs, check_vma=False)
```

time: 270 us -> 127 us (0.47)
  blocking collectives: 159 us -> 0 us
  Pallas kernels: 0 us -> 98.2 us
  waiting for transfers between devices: 30.7 us -> 0.01 us
  matrix products: 25.8 us -> 6.2 us
  local copies, waits for them, and re-layouts: 29.6 us -> 12.1 us
  between operations: 13.7 us -> 0.19 us
    all_to_all x2 -> x0, blocking collectives: 159 us -> none  [the longest x1 82.4 us: local(): lax.all_to_all(copies, ('seq', 'tp'), split_axis=0, concat_axis=0, tiled=...]
    pallas_call x0 -> x1, Pallas kernels: none -> 98.2 us  [moe(): pl.pallas_call(functools.partial(moe_kernel, n_seq, n_x), out_shape=jax.S...]
    reduce_scatter x1 -> x0, waiting for transfers between devices: 29.9 us -> none  [local(): lax.psum_scatter(jnp.dot(attended, w_out, preferred_element_type=jnp.floa...]
    dot_general x6 -> x0, matrix products: 19.4 us -> none  [the longest x2 10.3 us: one_expert(): jnp.einsum('vi,ipk->vpk', input_rows, gate_up_matrix, preferred_element_t...]
    another operation x5 -> x0, local copies, waits for them, and re-layouts: 12 us -> none  [the longest x2 10.2 us: one_expert(): input_rows = chosen.reshape(-1, MODEL_WIDTH)]
    slice x3 -> x0, local copies, waits for them, and re-layouts: 8.36 us -> none  [local(): gathered[:, :, expert]]
  transfers between devices with their start and end apart: 2 -> 2, of which waited for: 2 -> 0; matrix products, arithmetic and copies ran while one was open for 1% -> 7% of each run, Pallas kernels for 0% -> 0%
where the time goes in v1:
time: 127 us; the launch traced here: 126 us
  Pallas kernels  98.2 us (77%)
  local copies, waits for them, and re-layouts  12.1 us (10%)
  matrix products  6.2 us (5%)
  starting transfers between devices  5.41 us (4%)
  other arithmetic  4.1 us (3%)
    pallas_call x1, Pallas kernels, moe(): pl.pallas_call(functools.partial(moe_kernel, n_seq, n_x), out_shape=jax.S...  98.2 us
    ppermute x1, starting transfers between devices, from_behind(): lax.ppermute(value, axis, [(source, source + steps) for source in range(f...  4.37 us
    dot_general x1, matrix products, local(): jnp.einsum('td,dhc->thc', normed, w_qkv, preferred_element_type=jnp.float32)  3.77 us
    unnamed x13, local copies, waits for them, and re-layouts  3.67 us
  transfers between devices with their start and end apart: 2, of which 0 were waited for; matrix products, arithmetic and copies ran while one was open for 7% of the time, Pallas kernels for 0%

profile of v1, /device:TPU:1, one launch (start us, length us, event | category | flops | bytes accessed | tf_op | source)
XLA Modules:
  0.0 126.2 jit_solution(6389738895291252370)
XLA Ops:
  0.0 1.7 %fusion.2 = f32[128]{0:T(128)S(1)} fusion(bf16[128,2880]{0,1:T(8,128)(2,1)} %param.10), kind=kLoop, calls=%fused_computation.5 | loop fusion | flops 1105792 | bytes 737792 | tf_op jit(solution)/shard_map/reduce_sum | solution.py:29
  1.7 0.0 copy-start.2
  1.7 3.8 %fusion.7 = bf16[128,640]{1,0:T(8,128)(2,1)S(1)} fusion(bf16[2880,1,640]{2,0,1:T(8,128)(2,1)} %param.12, bf16[128,2880]{0,1:T(8,128)(2,1)} %param.10, f32[2880]{0:T(1024)} %param.11, f32[128]{0:T(128)S(1)} %add_rsqrt_fusion), kind=kOutput, calls=%fused_computation.11 | convolution fusion | flops 473415680 | bytes 4599552 | tf_op jit(solution)/shard_map/td,dhc->thc/dot_general | solution.py:418
  5.5 0.2 copy.32
  5.7 4.4 %collective-permute-start = (bf16[128,1,128]{0,2,1:T(8,128)(2,1)S(1)}, bf16[128,1,128]{0,2,1:T(8,128)(2,1)S(1)}, u32[]{:S(2)}, u32[]{:S(2)}) collective-permute-start(bf16[128,1,128]{0,2,1:T(8,128)(2,1)S(1)} %pad_maximum_fusion), channel_id=1, source_target_pairs={{0,8},{8,16},{16,24},{24,32},{32,40},{40,48},{48,56},{56,64},{64,7... | collective-permute-start | bytes 98312 | tf_op jit(solution)/shard_map/ppermute | solution.py:25
  10.1 0.0 copy-done.4
  10.1 1.0 collective-permute-start.1
  11.2 0.6 compare_convert_fusion.1
  11.8 2.2 %constant_dynamic-slice_fusion = bf16[16,2880]{0,1:T(8,128)(2,1)} fusion(bf16[128,2880]{0,1:T(8,128)(2,1)} %param.10, s32[]{:T(128)S(6)} %select_n.37), kind=kLoop, calls=%fused_computation.52 | loop fusion | bytes 184324 | tf_op jit(solution)/shard_map/dynamic_slice | solution.py:447
  14.0 0.0 copy-done.1
  14.0 0.1 copy.33
  14.1 2.0 %copy.44.stream_rows = bf16[16,2880]{1,0:T(8,128)(2,1)} copy(bf16[16,2880]{0,1:T(8,128)(2,1)} %constant_dynamic-slice_fusion) | data formatting | bytes 184320
  16.1 0.6 broadcast_in_dim.22.gain
  16.8 0.0 collective-permute-done.1
  16.8 0.1 fusion.19
  16.9 0.1 copy.40
  17.0 0.1 copy.39
  17.1 0.1 copy.38
  17.2 0.8 multiply_multiply_fusion
  18.0 0.1 mul.95
  18.1 0.1 copy.41
  18.2 0.6 pad_maximum_fusion.1.picker
  18.8 0.7 convert_element_type.77
  19.5 0.0 collective-permute-done
  19.6 0.3 fusion.30
  19.9 0.2 fusion.10
  20.0 0.3 convolution_convert_fusion.1
  20.4 1.8 %convolution_convert_fusion = bf16[128,2880]{0,1:T(8,128)(2,1)} fusion(bf16[512,2880]{0,1:T(8,128)(2,1)S(1)} %copy-done, bf16[128,512]{0,1:T(8,128)(2,1)S(1)} %bitcast.60), kind=kOutput, calls=%fused_computation.2 | convolution fusion | flops 377856000 | bytes 3817472 | tf_op jit(solution)/shard_map/dot_general | solution.py:445
  22.2 2.3 %copy.35 = bf16[128,2880]{1,0:T(8,128)(2,1)} copy(bf16[128,2880]{0,1:T(8,128)(2,1)} %convolution_convert_fusion) | data formatting | bytes 1474560 | tf_op jit(solution)/shard_map/convert_element_type | solution.py:445
  24.4 2.0 %copy.46 = bf16[4,2,16,2880]{3,2,0,1:T(8,128)(2,1)} copy(bf16[4,2,16,2880]{3,2,1,0:T(8,128)(2,1)} %bitcast.56) | data formatting | bytes 1474560 | tf_op jit(solution)/shard_map/reshape | solution.py:446
  26.5 98.2 %shard_map.100 = bf16[16,2880]{1,0:T(8,128)(2,1)} custom-call(bf16[2,4,16,2880]{3,2,1,0:T(8,128)(2,1)} %bitcast.55, bf16[16,2880]{1,0:T(8,128)(2,1)} %copy.44.stream_rows, f32[1,2880]{1,0:T(1,128)} %broadcast_in_dim.22.gain, bf16[128,32]{1,0:T(8,128)(2,1)} %bitcast.59, bf16[96,128]{1,0:T(8,128)(2,1)} %pad_maximum_fusion.1.picker, ...), custom_call_target="tpu_custom_call" | custom-call | tf_op jit(solution)/shard_map/pallas_call | solution.py:359
  124.7 1.5 %copy.48 = bf16[16,2880]{1,0:T(8,128)(2,1)} copy(bf16[16,2880]{1,0:T(8,128)(2,1)} %shard_map.100) | data formatting | bytes 184320
  (22 shorter events, 0.2 us)
Async XLA Ops:
  0.0 20.4 %copy-start = (bf16[512,2880]{0,1:T(8,128)(2,1)S(1)}, bf16[512,2880]{0,1:T(8,128)(2,1)}, u32[]{:S(2)}) copy-start(bf16[512,2880]{0,1:T(8,128)(2,1)} %param.14) | copy-start | bytes 8847364
  0.0 10.0 %copy-start.3 = (s32[16,4]{0,1:T(4,128)S(1)}, s32[16,4]{0,1:T(4,128)}, u32[]{:S(2)}) copy-start(s32[16,4]{0,1:T(4,128)} %param.16) | copy-start | bytes 772
  0.0 10.1 %copy-start.4 = (f32[16,4]{0,1:T(4,128)S(1)}, f32[16,4]{0,1:T(4,128)}, u32[]{:S(2)}) copy-start(f32[16,4]{0,1:T(4,128)} %param.17) | copy-start | bytes 772
  1.7 12.3 %copy-start.1 = (bf16[128,1,128]{2,0,1:T(8,128)(2,1)S(1)}, bf16[128,1,128]{2,0,1:T(8,128)(2,1)}, u32[]{:S(2)}) copy-start(bf16[128,1,128]{2,0,1:T(8,128)(2,1)} %param.13) | copy-start | bytes 98308
  1.7 14.5 %copy-start.2 = (f32[2880]{0:T(1024)S(1)}, f32[2880]{0:T(1024)}, u32[]{:S(2)}) copy-start(f32[2880]{0:T(1024)} %param.15) | copy-start | bytes 34564
  5.7 13.9 %collective-permute-start = (bf16[128,1,128]{0,2,1:T(8,128)(2,1)S(1)}, bf16[128,1,128]{0,2,1:T(8,128)(2,1)S(1)}, u32[]{:S(2)}, u32[]{:S(2)}) collective-permute-start(bf16[128,1,128]{0,2,1:T(8,128)(2,1)S(1)} %pad_maximum_fusion), channel_id=1, source_target_pairs={{0,8},{8,16},{16,24},{24,32},{32,40},{40,48},{48,56},{56,64},{64,7... | collective-permute-start | bytes 98312 | tf_op jit(solution)/shard_map/ppermute | solution.py:25
  10.1 6.7 %collective-permute-start.1 = (f32[16,8]{0,1:T(8,128)S(1)}, f32[16,8]{0,1:T(8,128)S(1)}, u32[]{:S(2)}, u32[]{:S(2)}) collective-permute-start(f32[16,8]{0,1:T(8,128)S(1)} %get-tuple-element.19), channel_id=1, source_target_pairs={{0,1},{1,0},{2,3},{3,2},{4,5},{5,4},{6,7},{7,6},{8,9},{9,8},{10,11... | collective-permute-start | bytes 1544 | tf_op jit(solution)/shard_map/ppermute | solution.py:376

commit v2 on v0

v2 whole, which is shorter than its diff:
```python
import functools

import jax
import jax.numpy as jnp
from jax import lax
from jax.experimental import pallas as pl
from jax.experimental.pallas import tpu as pltpu
from jax.sharding import PartitionSpec as P

HEAD_SIZE = 64
WINDOW_KEYS = 128
TOPK = 4
EPS = 1e-05
MESH = pl.DeviceIdType.MESH
BF16, F32 = jnp.bfloat16, jnp.float32


def rms_scale(values, gain_vec):
    mean_sq = jnp.mean(values * values, axis=-1, keepdims=True)
    return values * lax.rsqrt(mean_sq + EPS) * gain_vec


def contract_last(a, b):
    return lax.dot_general(a, b, (((1,), (1,)), ((), ())), preferred_element_type=F32)


def contract_first(a, b):
    return lax.dot_general(a, b, (((0,), (0,)), ((), ())), preferred_element_type=F32)


class Copies:
    def __init__(self, send_sems):
        self.send_sems = send_sems
        self.started = []

    def start(self, src, dst, recv_sem, seq, tp):
        copy = pltpu.make_async_remote_copy(
            src_ref=src,
            dst_ref=dst,
            send_sem=self.send_sems.at[len(self.started)],
            recv_sem=recv_sem,
            device_id=(seq, tp),
            device_id_type=MESH,
        )
        copy.start()
        self.started.append(copy)

    def drain(self):
        for copy in self.started:
            copy.wait_send()


def arrived(ref, sem):
    pltpu.make_async_copy(ref, ref, sem).wait()


def window_attention(projected, earlier):
    length = projected.shape[0]
    pairs = projected.shape[1] // 128 - 1
    keyval = jnp.concatenate([earlier, projected[:, pairs * 128 :]], axis=0).astype(F32)
    swapped = pltpu.roll(keyval, 64, 1)
    low = lax.broadcasted_iota(jnp.int32, keyval.shape, 1) < HEAD_SIZE
    keys = [jnp.where(low, keyval, 0.0).astype(BF16), jnp.where(low, 0.0, swapped).astype(BF16)]
    values = [jnp.where(low, swapped, 0.0).astype(BF16), jnp.where(low, 0.0, keyval).astype(BF16)]
    queries = jnp.concatenate(
        [projected[:, pair * 128 : (pair + 1) * 128] for pair in range(pairs)], axis=0
    )
    shape = (queries.shape[0], keyval.shape[0])
    row = lax.broadcasted_iota(jnp.int32, shape, 0) % length
    offset = lax.broadcasted_iota(jnp.int32, shape, 1) - row
    in_window = (offset >= 1) & (offset <= WINDOW_KEYS)
    attended = None
    for side in range(2):
        scores = contract_last(queries, keys[side]) * HEAD_SIZE ** (-0.5)
        scores = jnp.where(in_window, scores, -1e30)
        exponent = jnp.exp(scores - jnp.max(scores, axis=-1, keepdims=True))
        weights = (exponent / jnp.sum(exponent, axis=-1, keepdims=True)).astype(BF16)
        term = jnp.dot(weights, values[side], preferred_element_type=F32)
        attended = term if attended is None else attended + term
    attended = attended.astype(BF16)
    return jnp.concatenate(
        [attended[pair * length : (pair + 1) * length] for pair in range(pairs)], axis=1
    )


def slot_table(route, core, n_seq, slot_core):
    count = route.shape[1]
    shape = (n_seq * 8, count)
    line = lax.broadcasted_iota(jnp.int32, shape, 0)
    expert = (line // 8 * 2 + core).astype(F32)
    chosen = jnp.zeros(shape, F32)
    weight = jnp.zeros(shape, F32)
    for k in range(TOPK):
        named = expert == route[k : k + 1, :]
        chosen = chosen + named.astype(F32)
        weight = weight + jnp.where(named, route[TOPK + k : TOPK + k + 1, :], 0.0)
    before = lax.broadcasted_iota(jnp.int32, (count, count), 0) < lax.broadcasted_iota(
        jnp.int32, (count, count), 1
    )
    rank = jnp.dot(chosen.astype(BF16), before.astype(BF16), preferred_element_type=F32)
    place = (line % 4).astype(F32)
    here = line % 8 // 4 == slot_core
    hit = jnp.where(here & (rank == place), chosen, 0.0)
    return hit.astype(BF16), hit * weight


def split3(values):
    high = values.astype(BF16)
    rest = values - high.astype(F32)
    middle = rest.astype(BF16)
    return high, middle, (rest - middle.astype(F32)).astype(BF16)


def layer_kernel(
    n_seq,
    n_x,
    route_own,
    attn_gain,
    mlp_gain,
    cache,
    stream_hbm,
    w_qkv_hbm,
    w_out_hbm,
    w_gateup_hbm,
    w_down_hbm,
    out,
    stream_t,
    w_qkv,
    w_out,
    tail,
    earlier,
    stream,
    route,
    part,
    attn_pair,
    attn_sum,
    attn_opp,
    attn_in,
    residual,
    hidden,
    packed,
    rows,
    w_gateup,
    w_down,
    product,
    from_pair,
    chip_sum,
    ring_opp,
    ring_in,
    final,
    returned,
    mixed,
    mixed_in,
    load_sems,
    send_sems,
    attn_sems,
    block_sems,
    ring_sems,
    pair_sems,
    back_sems,
    opp_sems,
    in_sems,
    home_sems,
):
    seq, tp = lax.axis_index("seq"), lax.axis_index("tp")
    x, core = tp // 2, tp % 2
    nz = 4 if n_seq % 4 == 0 else n_seq
    ny = n_seq // nz
    y, z = seq // nz, seq % nz
    partner = tp + 1 - 2 * core
    right_x, left_x, far_x = (x + 1) % n_x, (x + n_x - 1) % n_x, (x + 2) % n_x
    right, left, far = right_x * 2 + core, left_x * 2 + core, far_x * 2 + core
    chunk = max(1, n_seq // 4)
    chunks = n_seq // chunk
    half = chunks // 2
    y_steps = [0, 2, 1, 3] if ny == 4 else list(range(ny))
    first_order = [0, 2, 3, 1] if chunks == 4 else list(range(chunks))
    low_order = list(range(half))[::-1]
    high_order = list(range(half, chunks))
    width = out.shape[-1]
    length = stream.shape[0] * stream.shape[1]
    copies = Copies(send_sems)

    def load(src, dst, index):
        copy = pltpu.make_async_copy(src, dst, load_sems.at[index])
        copy.start()
        return copy

    edges = [0, width // 3 // 128 * 128, width * 2 // 3 // 128 * 128, width]
    spans = [pl.ds(a, b - a) for a, b in zip(edges[:-1], edges[1:]) if b > a]
    stream_load = load(stream_hbm, stream_t, 0)
    qkv_loads = [
        load(w_qkv_hbm.at[span], w_qkv.at[span], 1 + i) for i, span in enumerate(spans)
    ]
    out_load = load(w_out_hbm, w_out, 4)

    def behind(slot):
        dy, dz = y_steps[slot // nz], slot % nz
        return ((y + ny - dy) % ny) * nz + (z + nz - dz) % nz

    def ahead(slot):
        dy, dz = y_steps[slot // nz], slot % nz
        return ((y + dy) % ny) * nz + (z + dz) % nz

    barrier = pltpu.get_barrier_semaphore()
    after = (seq + 1) % n_seq
    for slot in range(1, n_seq):
        pl.semaphore_signal(barrier, inc=1, device_id=(ahead(slot), tp), device_id_type=MESH)
    for peer in (partner, right, left):
        pl.semaphore_signal(barrier, inc=1, device_id=(seq, peer), device_id_type=MESH)
    route[core] = route_own[...]

    square = lax.broadcasted_iota(jnp.int32, (length, length), 0)
    eye = (square == lax.broadcasted_iota(jnp.int32, (length, length), 1)).astype(BF16)
    stream_load.wait()
    tokens = contract_last(eye, stream_t[...])
    stream[...] = tokens.astype(BF16).reshape(stream.shape)
    normed = rms_scale(tokens, attn_gain[...]).astype(BF16)
    projected = None
    for span, (a, b), copy in zip(spans, zip(edges[:-1], edges[1:]), qkv_loads):
        copy.wait()
        term = jnp.dot(normed[:, a:b], w_qkv[span], preferred_element_type=F32)
        projected = term if projected is None else projected + term
    projected = projected.astype(BF16)
    tail[...] = projected[:, projected.shape[1] - 128 :]
    pl.semaphore_wait(barrier, n_seq - 1 + 3)
    copies.start(tail, earlier, attn_sems.at[0], after, tp)
    copies.start(route.at[core], route.at[core], attn_sems.at[1], seq, partner)
    arrived(earlier, attn_sems.at[0])
    attended = window_attention(projected, jnp.where(seq == 0, cache[...], earlier[...]))
    out_load.wait()
    weight_loads = [load(w_gateup_hbm, w_gateup, 5), load(w_down_hbm, w_down, 6)]
    part[...] = contract_last(attended, w_out[...]).reshape(part.shape).astype(BF16)

    copies.start(part.at[:, 1 - core], attn_pair, attn_sems.at[2], seq, partner)
    arrived(route.at[1 - core], attn_sems.at[1])
    tables = [slot_table(route[c], core, n_seq, c) for c in range(2)]
    arrived(attn_pair, attn_sems.at[2])

    def pair_total(peer_x):
        return part[peer_x, core].astype(F32) + attn_pair[peer_x].astype(F32)

    attn_sum[far_x] = pair_total(far_x).astype(BF16)
    copies.start(attn_sum.at[far_x, 0], attn_opp.at[0], attn_sems.at[3], seq, right)
    copies.start(attn_sum.at[far_x, 1], attn_opp.at[1], attn_sems.at[4], seq, left)
    attn_sum[right_x] = pair_total(right_x).astype(BF16)
    copies.start(attn_sum.at[right_x, 1], attn_in.at[0, 1], attn_sems.at[5], seq, right)
    attn_sum[left_x] = pair_total(left_x).astype(BF16)
    copies.start(attn_sum.at[left_x, 0], attn_in.at[1, 0], attn_sems.at[6], seq, left)
    total = stream[tp].astype(F32).reshape(2, -1, width) + pair_total(x)
    arrived(attn_opp.at[0], attn_sems.at[3])
    attn_sum[right_x, 0] = (
        attn_sum[right_x, 0].astype(F32) + attn_opp[0].astype(F32)
    ).astype(BF16)
    copies.start(attn_sum.at[right_x, 0], attn_in.at[0, 0], attn_sems.at[7], seq, right)
    arrived(attn_opp.at[1], attn_sems.at[4])
    attn_sum[left_x, 1] = (
        attn_sum[left_x, 1].astype(F32) + attn_opp[1].astype(F32)
    ).astype(BF16)
    copies.start(attn_sum.at[left_x, 1], attn_in.at[1, 1], attn_sems.at[8], seq, left)
    for which, part_of, sem in ((0, 1, 5), (1, 0, 6), (0, 0, 7), (1, 1, 8)):
        arrived(attn_in.at[which, part_of], attn_sems.at[sem])
    total = (total + attn_in[0].astype(F32) + attn_in[1].astype(F32)).reshape(-1, width)
    residual[...] = total
    hidden[core] = rms_scale(total, mlp_gain[...]).astype(BF16)
    copies.start(hidden.at[core], hidden.at[core], attn_sems.at[9], seq, partner)
    arrived(hidden.at[1 - core], attn_sems.at[9])

    packed[...] = (
        (
            jnp.dot(tables[0][0], hidden[0], preferred_element_type=F32)
            + jnp.dot(tables[1][0], hidden[1], preferred_element_type=F32)
        )
        .reshape(packed.shape)
        .astype(BF16)
    )
    for group in first_order:
        for slot in range(group * chunk, (group + 1) * chunk):
            if slot:
                copies.start(
                    packed.at[behind(slot)],
                    rows.at[core, x, slot],
                    block_sems.at[group],
                    behind(slot),
                    tp,
                )
    rows[core, x, 0] = packed[seq]

    def slots(group):
        return pl.ds(group * chunk, chunk)

    def spread(group):
        first = 1 if group == 0 else 0
        if chunk > first:
            got = rows.at[core, x, pl.ds(group * chunk + first, chunk - first)]
            arrived(got, block_sems.at[group])
        own = rows.at[core, x, slots(group)]
        copies.start(own, own, ring_sems.at[0, group], seq, right)
        copies.start(own, own, ring_sems.at[1, group], seq, left)
        copies.start(own, own, pair_sems.at[0, group], seq, partner)

    done = set()

    def take(from_left, group):
        if (from_left, group) in done:
            return
        done.add((from_left, group))
        got = rows.at[core, left_x if from_left else right_x, slots(group)]
        arrived(got, ring_sems.at[0 if from_left else 1, group])
        if from_left and group < half:
            copies.start(got, got, ring_sems.at[2, group], seq, right)
        if not from_left and group >= half:
            copies.start(got, got, ring_sems.at[2, group], seq, left)
        copies.start(got, got, pair_sems.at[1 if from_left else 2, group], seq, partner)

    def compute(block_x, which, expert):
        taken = rows[expert, block_x].reshape(n_seq * 8, width)
        gate = contract_last(taken, w_gateup[expert, 0])
        up = contract_last(taken, w_gateup[expert, 1])
        activated = (gate / (1.0 + jnp.exp(-gate)) * up).astype(BF16)
        result = jnp.dot(activated, w_down[expert], preferred_element_type=F32)
        product[expert, block_x] = result.reshape(n_seq, 8, width).astype(BF16)

    def block(block_x, which):
        for group in range(chunks):
            arrived(rows.at[1 - core, block_x, slots(group)], pair_sems.at[which, group])
        compute(block_x, which, 1 - core)
        for group in range(chunks):
            copies.start(
                product.at[1 - core, block_x, slots(group)],
                from_pair.at[block_x, slots(group)],
                back_sems.at[which, group],
                seq,
                partner,
            )
        compute(block_x, which, core)

    def pair_sum(block_x, which, group):
        at = slots(group)
        arrived(from_pair.at[block_x, at], back_sems.at[which, group])
        chip_sum[block_x, at] = (
            product[core, block_x, at].astype(F32) + from_pair[block_x, at].astype(F32)
        ).astype(BF16)

    for group in first_order[:-1]:
        spread(group)
    take(True, 0)
    if half in first_order[:-1]:
        take(False, half)
    spread(first_order[-1])
    take(False, chunks - 1)
    for copy in weight_loads:
        copy.wait()
    block(x, 0)
    for group in range(chunks):
        take(True, first_order[group])
        take(False, first_order[group])
    block(left_x, 1)
    block(right_x, 2)
    for group in high_order:
        pair_sum(right_x, 2, group)
        copies.start(
            chip_sum.at[right_x, slots(group)],
            ring_in.at[0, slots(group)],
            in_sems.at[0, group],
            seq,
            right,
        )
    for group in low_order:
        pair_sum(left_x, 1, group)
        copies.start(
            chip_sum.at[left_x, slots(group)],
            ring_in.at[1, slots(group)],
            in_sems.at[1, group],
            seq,
            left,
        )

    for group in range(chunks):
        got = rows.at[core, far_x, slots(group)]
        arrived(got, ring_sems.at[2, group])
        copies.start(got, got, pair_sems.at[3, group], seq, partner)
    block(far_x, 3)
    for low, high in zip(low_order, high_order):
        pair_sum(far_x, 3, low)
        copies.start(
            chip_sum.at[far_x, slots(low)], ring_opp.at[slots(low)], opp_sems.at[low], seq, right
        )
        pair_sum(far_x, 3, high)
        copies.start(
            chip_sum.at[far_x, slots(high)], ring_opp.at[slots(high)], opp_sems.at[high], seq, left
        )
    for low, high in zip(low_order, high_order):
        pair_sum(right_x, 2, low)
        pair_sum(left_x, 1, high)
        pair_sum(x, 0, low)
        pair_sum(x, 0, high)
    for low, high in zip(low_order, high_order):
        for group, peer_x, peer, side in ((low, right_x, right, 0), (high, left_x, left, 1)):
            at = slots(group)
            arrived(ring_opp.at[at], opp_sems.at[group])
            chip_sum[peer_x, at] = (
                chip_sum[peer_x, at].astype(F32) + ring_opp[at].astype(F32)
            ).astype(BF16)
            copies.start(
                chip_sum.at[peer_x, at], ring_in.at[side, at], in_sems.at[side, group], seq, peer
            )

    for low, high in zip(low_order, high_order):
        for group in (low, high):
            at = slots(group)
            arrived(ring_in.at[0, at], in_sems.at[0, group])
            arrived(ring_in.at[1, at], in_sems.at[1, group])
            final[at] = (
                chip_sum[x, at].astype(F32)
                + ring_in[0, at].astype(F32)
                + ring_in[1, at].astype(F32)
            ).astype(BF16)
            for slot in range(group * chunk, (group + 1) * chunk):
                if slot:
                    copies.start(
                        final.at[slot], returned.at[seq], home_sems.at[slot], ahead(slot), tp
                    )
    returned[seq] = final[0]
    pickers = [split3(table[1]) for table in tables]
    for slot in range(1, n_seq):
        arrived(returned.at[behind(slot)], home_sems.at[slot])
    terms = returned[...].reshape(n_seq * 8, width)
    for c in range(2):
        mixed[c] = sum(contract_first(piece, terms) for piece in pickers[c])
    copies.start(mixed.at[1 - core], mixed_in, attn_sems.at[10], seq, partner)
    arrived(mixed_in, attn_sems.at[10])
    out[...] = (residual[...] + (mixed[core] + mixed_in[...])).astype(BF16)
    copies.drain()


def local(
    stream_in,
    attn_gain,
    w_qkv,
    key_value_cache,
    w_out,
    mlp_gain,
    expert_index,
    gate_weight,
    w_gateup,
    w_down,
):
    n_seq = lax.axis_size("seq")
    n_tp = lax.axis_size("tp")
    n_x = n_tp // 2
    length, width = stream_in.shape
    count = length // n_tp
    hidden = w_down.shape[1]
    columns = w_qkv.shape[2]
    heads_width = w_out.shape[0]
    route = jnp.concatenate([expert_index.astype(F32), gate_weight], axis=1).T
    vmem, dma = pltpu.VMEM, pltpu.SemaphoreType.DMA
    chunks = n_seq // max(1, n_seq // 4)
    scratch = [
        vmem((width, length), BF16),
        vmem((width, columns), BF16),
        vmem((width, heads_width), BF16),
        vmem((length, 128), BF16),
        vmem((length, 128), BF16),
        vmem((n_tp, count, width), BF16),
        vmem((2, 2 * TOPK, count), F32),
        vmem((n_x, 2, 2, count // 2, width), BF16),
        vmem((n_x, 2, count // 2, width), BF16),
        vmem((n_x, 2, count // 2, width), BF16),
        vmem((2, count // 2, width), BF16),
        vmem((2, 2, count // 2, width), BF16),
        vmem((count, width), F32),
        vmem((2, count, width), BF16),
        vmem((n_seq, 8, width), BF16),
        vmem((2, n_x, n_seq, 8, width), BF16),
        vmem((2, 2, hidden, width), BF16),
        vmem((2, hidden, width), BF16),
        vmem((2, n_x, n_seq, 8, width), BF16),
        vmem((n_x, n_seq, 8, width), BF16),
        vmem((n_x, n_seq, 8, width), BF16),
        vmem((n_seq, 8, width), BF16),
        vmem((2, n_seq, 8, width), BF16),
        vmem((n_seq, 8, width), BF16),
        vmem((n_seq, 8, width), BF16),
        vmem((2, count, width), F32),
        vmem((count, width), F32),
        dma((7,)),
        dma((160,)),
        dma((11,)),
        dma((chunks,)),
        dma((3, chunks)),
        dma((4, chunks)),
        dma((4, chunks)),
        dma((chunks,)),
        dma((2, chunks)),
        dma((n_seq,)),
    ]
    in_vmem = pl.BlockSpec(memory_space=pltpu.VMEM)
    return pl.pallas_call(
        functools.partial(layer_kernel, n_seq, n_x),
        out_shape=jax.ShapeDtypeStruct((count, width), BF16),
        in_specs=[in_vmem] * 4 + [pl.BlockSpec(memory_space=pl.ANY)] * 5,
        out_specs=in_vmem,
        scratch_shapes=scratch,
        compiler_params=pltpu.CompilerParams(
            collective_id=0, has_side_effects=True, vmem_limit_bytes=63 * 1024 * 1024
        ),
    )(
        route,
        attn_gain[None],
        mlp_gain[None],
        key_value_cache.reshape(length, 128),
        stream_in.T,
        w_qkv.reshape(width, columns),
        w_out.T,
        w_gateup.transpose(0, 2, 3, 1),
        w_down,
    )


def solution(mesh):
    in_specs = (
        P("seq", None),
        P(),
        P(None, "tp", None),
        P(None, "tp", None),
        P("tp", None),
        P(),
        P(("seq", "tp"), None),
        P(("seq", "tp"), None),
        P("seq", None, None, "tp"),
        P("seq", "tp", None),
    )
    out_specs = P(("seq", "tp"), None)
    return jax.shard_map(local, mesh=mesh, in_specs=in_specs, out_specs=out_specs, check_vma=False)
```

time: 270 us -> 112 us (0.41)
  blocking collectives: 159 us -> 0 us
  Pallas kernels: 0 us -> 104 us
  waiting for transfers between devices: 30.7 us -> 0 us
  matrix products: 25.8 us -> 0 us
  local copies, waits for them, and re-layouts: 29.6 us -> 4.16 us
  between operations: 13.7 us -> 0.01 us
  starting transfers between devices: 4.37 us -> 0 us
  other arithmetic: 5.97 us -> 1.96 us
    all_to_all x2 -> x0, blocking collectives: 159 us -> none  [the longest x1 82.4 us: local(): lax.all_to_all(copies, ('seq', 'tp'), split_axis=0, concat_axis=0, tiled=...]
    pallas_call x0 -> x1, Pallas kernels: none -> 104 us  [local(): pl.pallas_call(functools.partial(layer_kernel, n_seq, n_x), out_shape=jax...]
    reduce_scatter x1 -> x0, waiting for transfers between devices: 29.9 us -> none  [local(): lax.psum_scatter(jnp.dot(attended, w_out, preferred_element_type=jnp.floa...]
    dot_general x10 -> x0, matrix products: 25.8 us -> none  [the longest x2 10.3 us: one_expert(): jnp.einsum('vi,ipk->vpk', input_rows, gate_up_matrix, preferred_element_t...]
    another operation x5 -> x0, local copies, waits for them, and re-layouts: 12 us -> none  [the longest x2 10.2 us: one_expert(): input_rows = chosen.reshape(-1, MODEL_WIDTH)]
    slice x4 -> x0, local copies, waits for them, and re-layouts: 8.36 us -> none  [the longest x3 8.36 us: local(): gathered[:, :, expert]]
    convert_element_type x5 -> x0, local copies, waits for them, and re-layouts: 5.25 us -> none  [the longest x1 3.33 us: local(): partials.astype(jnp.bfloat16)]
    ppermute x1 -> x0, starting transfers between devices: 4.37 us -> none  [from_behind(): lax.ppermute(value, axis, [(source, source + steps) for source in range(f...]
  transfers between devices with their start and end apart: 2 -> 0, of which waited for: 2 -> 0; matrix products, arithmetic and copies ran while one was open for 1% -> 0% of each run, Pallas kernels for 0% -> 0%
where the time goes in v2:
time: 112 us; the launch traced here: 111 us
  Pallas kernels  104 us (93%)
  local copies, waits for them, and re-layouts  4.16 us (4%)
  other arithmetic  1.96 us (2%)
    pallas_call x1, Pallas kernels, local(): pl.pallas_call(functools.partial(layer_kernel, n_seq, n_x), out_shape=jax...  104 us

profile of v2, /device:TPU:1, one launch (start us, length us, event | category | flops | bytes accessed | tf_op | source)
XLA Modules:
  0.0 110.6 jit_solution(3638653372635780463)
XLA Ops:
  0.0 0.7 convert_element_type.3
  0.7 1.3 %maximum_bitcast_fusion.route_own = f32[8,16]{1,0:T(8,128)} fusion(f32[16,4]{0,1:T(4,128)} %param.17, f32[16,4]{0,1:T(4,128)S(1)} %convert_element_type.3), kind=kLoop, calls=%fused_computation | loop fusion | flops 128 | bytes 1024 | tf_op jit(solution)/shard_map/transpose | solution.py:457
  2.0 1.3 %broadcast_in_dim.6.attn_gain = f32[1,2880]{1,0:T(1,128)} reshape(f32[2880]{0:T(1024)} %param.11) | data formatting | bytes 23040 | tf_op jit(solution)/shard_map/broadcast_in_dim | solution.py:511
  3.3 1.3 %broadcast_in_dim.7.mlp_gain = f32[1,2880]{1,0:T(1,128)} reshape(f32[2880]{0:T(1024)} %param.15) | data formatting | bytes 23040 | tf_op jit(solution)/shard_map/broadcast_in_dim | solution.py:512
  4.6 104.5 %shard_map.100 = bf16[16,2880]{1,0:T(8,128)(2,1)} custom-call(f32[8,16]{1,0:T(8,128)} %maximum_bitcast_fusion.route_own, f32[1,2880]{1,0:T(1,128)} %broadcast_in_dim.6.attn_gain, f32[1,2880]{1,0:T(1,128)} %broadcast_in_dim.7.mlp_gain, bf16[128,128]{1,0:T(8,128)(2,1)} %bitcast.11, bf16[2880,128]{1,0:T(8,128)(2,1)} %bitcast.10, bf16[2880,640]{1,0:T(8,128)(2,1)} %bitcast.8, ...), custom_call_target="tpu_custom_call" | custom-call | tf_op jit(solution)/shard_map/pallas_call | solution.py:500
  109.1 1.5 %copy.12 = bf16[16,2880]{1,0:T(8,128)(2,1)} copy(bf16[16,2880]{1,0:T(8,128)(2,1)} %shard_map.100) | data formatting | bytes 184320

commit v3 on v2

--- a/solution.py
+++ b/solution.py
@@ -54,32 +54,47 @@
     pltpu.make_async_copy(ref, ref, sem).wait()
 
 
-def window_attention(projected, earlier):
-    length = projected.shape[0]
-    pairs = projected.shape[1] // 128 - 1
-    keyval = jnp.concatenate([earlier, projected[:, pairs * 128 :]], axis=0).astype(F32)
+def key_value_sides(keyval):
+    keyval = keyval.astype(F32)
     swapped = pltpu.roll(keyval, 64, 1)
     low = lax.broadcasted_iota(jnp.int32, keyval.shape, 1) < HEAD_SIZE
     keys = [jnp.where(low, keyval, 0.0).astype(BF16), jnp.where(low, 0.0, swapped).astype(BF16)]
     values = [jnp.where(low, swapped, 0.0).astype(BF16), jnp.where(low, 0.0, keyval).astype(BF16)]
+    return keys, values
+
+
+def own_scores(projected):
+    length = projected.shape[0]
+    pairs = projected.shape[1] // 128 - 1
+    keys, values = key_value_sides(projected[:, pairs * 128 :])
     queries = jnp.concatenate(
         [projected[:, pair * 128 : (pair + 1) * 128] for pair in range(pairs)], axis=0
     )
-    shape = (queries.shape[0], keyval.shape[0])
+    shape = (queries.shape[0], length)
     row = lax.broadcasted_iota(jnp.int32, shape, 0) % length
-    offset = lax.broadcasted_iota(jnp.int32, shape, 1) - row
-    in_window = (offset >= 1) & (offset <= WINDOW_KEYS)
+    later = lax.broadcasted_iota(jnp.int32, shape, 1) > row
+    scores = [
+        jnp.where(later, -1e30, contract_last(queries, key) * HEAD_SIZE ** (-0.5)) for key in keys
+    ]
+    return queries, later, scores, values
+
+
+def window_attention(prepared, earlier):
+    queries, later, own, own_values = prepared
+    keys, values = key_value_sides(earlier)
     attended = None
     for side in range(2):
-        scores = contract_last(queries, keys[side]) * HEAD_SIZE ** (-0.5)
-        scores = jnp.where(in_window, scores, -1e30)
+        before = contract_last(queries, keys[side]) * HEAD_SIZE ** (-0.5)
+        scores = jnp.concatenate([jnp.where(later, before, -1e30), own[side]], axis=1)
         exponent = jnp.exp(scores - jnp.max(scores, axis=-1, keepdims=True))
         weights = (exponent / jnp.sum(exponent, axis=-1, keepdims=True)).astype(BF16)
-        term = jnp.dot(weights, values[side], preferred_element_type=F32)
+        both = jnp.concatenate([values[side], own_values[side]], axis=0)
+        term = jnp.dot(weights, both, preferred_element_type=F32)
         attended = term if attended is None else attended + term
     attended = attended.astype(BF16)
+    length = earlier.shape[0]
     return jnp.concatenate(
-        [attended[pair * length : (pair + 1) * length] for pair in range(pairs)], axis=1
+        [attended[at : at + length] for at in range(0, attended.shape[0], length)], axis=1
     )
 
 
@@ -114,7 +129,8 @@
 def layer_kernel(
     n_seq,
     n_x,
-    route_own,
+    index_own,
+    weight_own,
     attn_gain,
     mlp_gain,
     cache,
@@ -208,14 +224,15 @@
         pl.semaphore_signal(barrier, inc=1, device_id=(ahead(slot), tp), device_id_type=MESH)
     for peer in (partner, right, left):
         pl.semaphore_signal(barrier, inc=1, device_id=(seq, peer), device_id_type=MESH)
-    route[core] = route_own[...]
+    route[core, 0:TOPK] = index_own[...].astype(F32)
+    route[core, TOPK:] = weight_own[...]
 
     square = lax.broadcasted_iota(jnp.int32, (length, length), 0)
     eye = (square == lax.broadcasted_iota(jnp.int32, (length, length), 1)).astype(BF16)
     stream_load.wait()
     tokens = contract_last(eye, stream_t[...])
     stream[...] = tokens.astype(BF16).reshape(stream.shape)
-    normed = rms_scale(tokens, attn_gain[...]).astype(BF16)
+    normed = rms_scale(tokens, attn_gain[...].reshape(1, -1)).astype(BF16)
     projected = None
     for span, (a, b), copy in zip(spans, zip(edges[:-1], edges[1:]), qkv_loads):
         copy.wait()
@@ -226,8 +243,9 @@
     pl.semaphore_wait(barrier, n_seq - 1 + 3)
     copies.start(tail, earlier, attn_sems.at[0], after, tp)
     copies.start(route.at[core], route.at[core], attn_sems.at[1], seq, partner)
+    prepared = own_scores(projected)
     arrived(earlier, attn_sems.at[0])
-    attended = window_attention(projected, jnp.where(seq == 0, cache[...], earlier[...]))
+    attended = window_attention(prepared, jnp.where(seq == 0, cache[...], earlier[...]))
     out_load.wait()
     weight_loads = [load(w_gateup_hbm, w_gateup, 5), load(w_down_hbm, w_down, 6)]
     part[...] = contract_last(attended, w_out[...]).reshape(part.shape).astype(BF16)
@@ -262,7 +280,7 @@
         arrived(attn_in.at[which, part_of], attn_sems.at[sem])
     total = (total + attn_in[0].astype(F32) + attn_in[1].astype(F32)).reshape(-1, width)
     residual[...] = total
-    hidden[core] = rms_scale(total, mlp_gain[...]).astype(BF16)
+    hidden[core] = rms_scale(total, mlp_gain[...].reshape(1, -1)).astype(BF16)
     copies.start(hidden.at[core], hidden.at[core], attn_sems.at[9], seq, partner)
     arrived(hidden.at[1 - core], attn_sems.at[9])
 
@@ -454,7 +472,6 @@
     hidden = w_down.shape[1]
     columns = w_qkv.shape[2]
     heads_width = w_out.shape[0]
-    route = jnp.concatenate([expert_index.astype(F32), gate_weight], axis=1).T
     vmem, dma = pltpu.VMEM, pltpu.SemaphoreType.DMA
     chunks = n_seq // max(1, n_seq // 4)
     scratch = [
@@ -500,16 +517,17 @@
     return pl.pallas_call(
         functools.partial(layer_kernel, n_seq, n_x),
         out_shape=jax.ShapeDtypeStruct((count, width), BF16),
-        in_specs=[in_vmem] * 4 + [pl.BlockSpec(memory_space=pl.ANY)] * 5,
+        in_specs=[in_vmem] * 5 + [pl.BlockSpec(memory_space=pl.ANY)] * 5,
         out_specs=in_vmem,
         scratch_shapes=scratch,
         compiler_params=pltpu.CompilerParams(
             collective_id=0, has_side_effects=True, vmem_limit_bytes=63 * 1024 * 1024
         ),
     )(
-        route,
-        attn_gain[None],
-        mlp_gain[None],
+        expert_index.T,
+        gate_weight.T,
+        attn_gain,
+        mlp_gain,
         key_value_cache.reshape(length, 128),
         stream_in.T,
         w_qkv.reshape(width, columns),

time: 112 us -> 107 us (0.955)
  local copies, waits for them, and re-layouts: 4.16 us -> 1.54 us
  other arithmetic: 1.96 us -> 0 us
    broadcast_in_dim x2 -> x0, local copies, waits for them, and re-layouts: 2.63 us -> none  [the longest x1 1.31 us: local(): attn_gain[None]]
    transpose x1 -> x0, other arithmetic: 1.28 us -> none  [local(): route = jnp.concatenate([expert_index.astype(F32), gate_weight], axis=1).T]
where the time goes in v3:
time: 107 us; the launch traced here: 106 us
  Pallas kernels  105 us (98%)
  local copies, waits for them, and re-layouts  1.54 us (1%)
    pallas_call x1, Pallas kernels, local(): pl.pallas_call(functools.partial(layer_kernel, n_seq, n_x), out_shape=jax...  105 us

profile of v3, /device:TPU:1, one launch (start us, length us, event | category | flops | bytes accessed | tf_op | source)
XLA Modules:
  0.0 106.2 jit_solution(1355395001660156836)
XLA Ops:
  0.0 104.7 %shard_map.100 = bf16[16,2880]{1,0:T(8,128)(2,1)} custom-call(s32[4,16]{1,0:T(4,128)} %bitcast.12, f32[4,16]{1,0:T(4,128)} %bitcast.13, f32[2880]{0:T(1024)} %attn_gain.1, f32[2880]{0:T(1024)} %mlp_gain.1, bf16[128,128]{1,0:T(8,128)(2,1)} %bitcast.11, bf16[2880,128]{1,0:T(8,128)(2,1)} %bitcast.10, bf16[2880,640]{1,0:T(8,128)(2,1)} %bitcast.8, ...), custom_call_target="tpu_custom_call" | custom-call | tf_op jit(solution)/shard_map/pallas_call | solution.py:517
  104.7 1.5 %copy.12 = bf16[16,2880]{1,0:T(8,128)(2,1)} copy(bf16[16,2880]{1,0:T(8,128)(2,1)} %shard_map.100) | data formatting | bytes 184320

commit v4 on v3

--- a/solution.py
+++ b/solution.py
@@ -153,23 +153,37 @@
     attn_opp,
     attn_in,
     residual,
-    hidden,
-    packed,
+    hidden_a,
+    hidden_b,
+    packed_a,
+    packed_b,
     rows,
+    rows_b,
     w_gateup,
     w_down,
+    sums,
     product,
+    product_b,
     from_pair,
+    from_pair_b,
     chip_sum,
+    chip_b,
     ring_opp,
     ring_in,
     final,
     returned,
+    back_b,
+    mixed_b,
+    mixed_pair,
+    mixed_sum,
+    mixed_in_b,
     mixed,
     mixed_in,
     load_sems,
     send_sems,
     attn_sems,
+    route_sems,
+    hidden_sems,
     block_sems,
     ring_sems,
     pair_sems,
@@ -177,6 +191,7 @@
     opp_sems,
     in_sems,
     home_sems,
+    mix_sems,
 ):
     seq, tp = lax.axis_index("seq"), lax.axis_index("tp")
     x, core = tp // 2, tp % 2
@@ -194,6 +209,7 @@
     low_order = list(range(half))[::-1]
     high_order = list(range(half, chunks))
     width = out.shape[-1]
+    split = rows.shape[-1]
     length = stream.shape[0] * stream.shape[1]
     copies = Copies(send_sems)
 
@@ -218,14 +234,22 @@
         dy, dz = y_steps[slot // nz], slot % nz
         return ((y + dy) % ny) * nz + (z + dz) % nz
 
+    order = (x, left_x, right_x, far_x)
+
+    def peer(place, other):
+        return order[place] * 2 + (1 - core if other else core)
+
+    peers = [peer(place, other) for place in range(4) for other in (True, False)]
+    peers = peers[:1] + peers[2:]
+
     barrier = pltpu.get_barrier_semaphore()
     after = (seq + 1) % n_seq
     for slot in range(1, n_seq):
         pl.semaphore_signal(barrier, inc=1, device_id=(ahead(slot), tp), device_id_type=MESH)
-    for peer in (partner, right, left):
-        pl.semaphore_signal(barrier, inc=1, device_id=(seq, peer), device_id_type=MESH)
-    route[core, 0:TOPK] = index_own[...].astype(F32)
-    route[core, TOPK:] = weight_own[...]
+    for other in peers:
+        pl.semaphore_signal(barrier, inc=1, device_id=(seq, other), device_id_type=MESH)
+    route[tp, 0:TOPK] = index_own[...].astype(F32)
+    route[tp, TOPK:] = weight_own[...]
 
     square = lax.broadcasted_iota(jnp.int32, (length, length), 0)
     eye = (square == lax.broadcasted_iota(jnp.int32, (length, length), 1)).astype(BF16)
@@ -240,9 +264,10 @@
         projected = term if projected is None else projected + term
     projected = projected.astype(BF16)
     tail[...] = projected[:, projected.shape[1] - 128 :]
-    pl.semaphore_wait(barrier, n_seq - 1 + 3)
+    pl.semaphore_wait(barrier, n_seq - 1 + len(peers))
     copies.start(tail, earlier, attn_sems.at[0], after, tp)
-    copies.start(route.at[core], route.at[core], attn_sems.at[1], seq, partner)
+    for other in peers:
+        copies.start(route.at[tp], route.at[tp], route_sems.at[tp], seq, other)
     prepared = own_scores(projected)
     arrived(earlier, attn_sems.at[0])
     attended = window_attention(prepared, jnp.where(seq == 0, cache[...], earlier[...]))
@@ -251,8 +276,12 @@
     part[...] = contract_last(attended, w_out[...]).reshape(part.shape).astype(BF16)
 
     copies.start(part.at[:, 1 - core], attn_pair, attn_sems.at[2], seq, partner)
-    arrived(route.at[1 - core], attn_sems.at[1])
-    tables = [slot_table(route[c], core, n_seq, c) for c in range(2)]
+    for other in peers:
+        arrived(route.at[other], route_sems.at[other])
+    tables = [
+        [slot_table(route[order[place] * 2 + c], core, n_seq, c) for c in range(2)]
+        for place in range(4)
+    ]
     arrived(attn_pair, attn_sems.at[2])
 
     def pair_total(peer_x):
@@ -280,29 +309,43 @@
         arrived(attn_in.at[which, part_of], attn_sems.at[sem])
     total = (total + attn_in[0].astype(F32) + attn_in[1].astype(F32)).reshape(-1, width)
     residual[...] = total
-    hidden[core] = rms_scale(total, mlp_gain[...].reshape(1, -1)).astype(BF16)
-    copies.start(hidden.at[core], hidden.at[core], attn_sems.at[9], seq, partner)
-    arrived(hidden.at[1 - core], attn_sems.at[9])
-
-    packed[...] = (
-        (
-            jnp.dot(tables[0][0], hidden[0], preferred_element_type=F32)
-            + jnp.dot(tables[1][0], hidden[1], preferred_element_type=F32)
-        )
-        .reshape(packed.shape)
-        .astype(BF16)
-    )
+    normed = rms_scale(total, mlp_gain[...].reshape(1, -1)).astype(BF16)
+    hidden_a[core] = normed[:, :split]
+    hidden_b[tp] = normed[:, split:]
+    copies.start(hidden_a.at[core], hidden_a.at[core], attn_sems.at[9], seq, partner)
+    for other in peers:
+        copies.start(hidden_b.at[tp], hidden_b.at[tp], hidden_sems.at[tp], seq, other)
+    arrived(hidden_a.at[1 - core], attn_sems.at[9])
+
+    def pack(place, first, second):
+        both = jnp.dot(tables[place][0][0], first, preferred_element_type=F32) + jnp.dot(
+            tables[place][1][0], second, preferred_element_type=F32
+        )
+        return both.reshape(n_seq, 8, -1).astype(BF16)
+
+    packed_a[...] = pack(0, hidden_a[0], hidden_a[1])
     for group in first_order:
         for slot in range(group * chunk, (group + 1) * chunk):
             if slot:
+                holder = behind(slot)
                 copies.start(
-                    packed.at[behind(slot)],
-                    rows.at[core, x, slot],
-                    block_sems.at[group],
-                    behind(slot),
-                    tp,
+                    packed_a.at[holder], rows.at[core, x, slot], block_sems.at[0, group], holder, tp
                 )
-    rows[core, x, 0] = packed[seq]
+    rows[core, x, 0] = packed_a[seq]
+    for other in peers:
+        arrived(hidden_b.at[other], hidden_sems.at[other])
+    for place in range(4):
+        packed_b[:, place] = pack(
+            place, hidden_b[order[place] * 2], hidden_b[order[place] * 2 + 1]
+        )
+    for group in first_order:
+        for slot in range(group * chunk, (group + 1) * chunk):
+            if slot:
+                holder = behind(slot)
+                copies.start(
+                    packed_b.at[holder], rows_b.at[core, slot], block_sems.at[1, group], holder, tp
+                )
+    rows_b[core, 0] = packed_b[seq]
 
     def slots(group):
         return pl.ds(group * chunk, chunk)
@@ -311,7 +354,7 @@
         first = 1 if group == 0 else 0
         if chunk > first:
             got = rows.at[core, x, pl.ds(group * chunk + first, chunk - first)]
-            arrived(got, block_sems.at[group])
+            arrived(got, block_sems.at[0, group])
         own = rows.at[core, x, slots(group)]
         copies.start(own, own, ring_sems.at[0, group], seq, right)
         copies.start(own, own, ring_sems.at[1, group], seq, left)
@@ -331,27 +374,88 @@
             copies.start(got, got, ring_sems.at[2, group], seq, left)
         copies.start(got, got, pair_sems.at[1 if from_left else 2, group], seq, partner)
 
-    def compute(block_x, which, expert):
-        taken = rows[expert, block_x].reshape(n_seq * 8, width)
-        gate = contract_last(taken, w_gateup[expert, 0])
-        up = contract_last(taken, w_gateup[expert, 1])
+    def take_b(group):
+        first = 1 if group == 0 else 0
+        if chunk > first:
+            got = rows_b.at[core, pl.ds(group * chunk + first, chunk - first)]
+            arrived(got, block_sems.at[1, group])
+        own = rows_b.at[core, slots(group)]
+        copies.start(own, own, pair_sems.at[4, group], seq, partner)
+
+    def entered(place, expert, which):
+        taken = rows[expert, order[place]].reshape(n_seq * 8, split)
+        return contract_last(taken, w_gateup[expert, which, :, 0:split])
+
+    def enter(place):
+        for group in range(chunks):
+            arrived(rows.at[1 - core, order[place], slots(group)], pair_sems.at[place, group])
+
+    def early(place):
+        enter(place)
+
+        def one(expert, carry):
+            for which in range(2):
+                sums[expert, place, which] = entered(place, expert, which)
+            return carry
+
+        lax.fori_loop(0, 2, one, 0)
+
+    def finish(place, expert, gate, up):
+        taken = rows_b[expert, :, place].reshape(n_seq * 8, width - split)
+        gate = gate + contract_last(taken, w_gateup[expert, 0, :, split:])
+        up = up + contract_last(taken, w_gateup[expert, 1, :, split:])
         activated = (gate / (1.0 + jnp.exp(-gate)) * up).astype(BF16)
         result = jnp.dot(activated, w_down[expert], preferred_element_type=F32)
-        product[expert, block_x] = result.reshape(n_seq, 8, width).astype(BF16)
-
-    def block(block_x, which):
-        for group in range(chunks):
-            arrived(rows.at[1 - core, block_x, slots(group)], pair_sems.at[which, group])
-        compute(block_x, which, 1 - core)
+        result = result.reshape(n_seq, 8, width).astype(BF16)
+        product[expert, order[place]] = result[:, :, :split]
+        product_b[expert, :, place] = result[:, :, split:]
+
+    def block(place, ready):
+        def one(expert):
+            if ready:
+                gate, up = sums[expert, place, 0], sums[expert, place, 1]
+            else:
+                gate, up = entered(place, expert, 0), entered(place, expert, 1)
+            finish(place, expert, gate, up)
+
+        one(1 - core)
+        block_x = order[place]
         for group in range(chunks):
             copies.start(
                 product.at[1 - core, block_x, slots(group)],
                 from_pair.at[block_x, slots(group)],
-                back_sems.at[which, group],
+                back_sems.at[place, group],
                 seq,
                 partner,
             )
-        compute(block_x, which, core)
+        copies.start(
+            product_b.at[1 - core, :, place],
+            from_pair_b.at[:, place],
+            mix_sems.at[place],
+            seq,
+            partner,
+        )
+        one(core)
+
+    def pair_sum_b(places):
+        for place in places:
+            arrived(from_pair_b.at[:, place], mix_sems.at[place])
+            chip_b[:, place] = (
+                product_b[core, :, place].astype(F32) + from_pair_b[:, place].astype(F32)
+            ).astype(BF16)
+        span = pl.ds(places[0], len(places))
+        which = 0 if places[0] == 0 else 1
+        for group in first_order:
+            for slot in range(group * chunk, (group + 1) * chunk):
+                if slot:
+                    copies.start(
+                        chip_b.at[slot, span],
+                        back_b.at[seq, span],
+                        home_sems.at[1 + which, slot],
+                        ahead(slot),
+                        tp,
+                    )
+        back_b[seq, span] = chip_b[0, span]
 
     def pair_sum(block_x, which, group):
         at = slots(group)
@@ -369,12 +473,19 @@
     take(False, chunks - 1)
     for copy in weight_loads:
         copy.wait()
-    block(x, 0)
-    for group in range(chunks):
-        take(True, first_order[group])
-        take(False, first_order[group])
-    block(left_x, 1)
-    block(right_x, 2)
+    early(0)
+    for group in first_order:
+        take(True, group)
+        take(False, group)
+    for group in first_order:
+        take_b(group)
+    early(1)
+    early(2)
+    for group in first_order:
+        arrived(rows_b.at[1 - core, slots(group)], pair_sems.at[4, group])
+    block(0, True)
+    block(1, True)
+    block(2, True)
     for group in high_order:
         pair_sum(right_x, 2, group)
         copies.start(
@@ -398,7 +509,9 @@
         got = rows.at[core, far_x, slots(group)]
         arrived(got, ring_sems.at[2, group])
         copies.start(got, got, pair_sems.at[3, group], seq, partner)
-    block(far_x, 3)
+    pair_sum_b((0, 1, 2))
+    enter(3)
+    block(3, False)
     for low, high in zip(low_order, high_order):
         pair_sum(far_x, 3, low)
         copies.start(
@@ -413,42 +526,81 @@
         pair_sum(left_x, 1, high)
         pair_sum(x, 0, low)
         pair_sum(x, 0, high)
+    pair_sum_b((3,))
     for low, high in zip(low_order, high_order):
-        for group, peer_x, peer, side in ((low, right_x, right, 0), (high, left_x, left, 1)):
+        for group, peer_x, target, side in ((low, right_x, right, 0), (high, left_x, left, 1)):
             at = slots(group)
             arrived(ring_opp.at[at], opp_sems.at[group])
             chip_sum[peer_x, at] = (
                 chip_sum[peer_x, at].astype(F32) + ring_opp[at].astype(F32)
             ).astype(BF16)
             copies.start(
-                chip_sum.at[peer_x, at], ring_in.at[side, at], in_sems.at[side, group], seq, peer
+                chip_sum.at[peer_x, at], ring_in.at[side, at], in_sems.at[side, group], seq, target
             )
 
-    for low, high in zip(low_order, high_order):
-        for group in (low, high):
-            at = slots(group)
-            arrived(ring_in.at[0, at], in_sems.at[0, group])
-            arrived(ring_in.at[1, at], in_sems.at[1, group])
-            final[at] = (
-                chip_sum[x, at].astype(F32)
-                + ring_in[0, at].astype(F32)
-                + ring_in[1, at].astype(F32)
-            ).astype(BF16)
-            for slot in range(group * chunk, (group + 1) * chunk):
-                if slot:
-                    copies.start(
-                        final.at[slot], returned.at[seq], home_sems.at[slot], ahead(slot), tp
-                    )
+    pickers = [[split3(tables[place][c][1]) for c in range(2)] for place in range(4)]
+
+    def mixture(place, c, terms):
+        return sum(contract_first(piece, terms) for piece in pickers[place][c])
+
+    def home(group):
+        at = slots(group)
+        arrived(ring_in.at[0, at], in_sems.at[0, group])
+        arrived(ring_in.at[1, at], in_sems.at[1, group])
+        final[at] = (
+            chip_sum[x, at].astype(F32) + ring_in[0, at].astype(F32) + ring_in[1, at].astype(F32)
+        ).astype(BF16)
+        for slot in range(group * chunk, (group + 1) * chunk):
+            if slot:
+                copies.start(
+                    final.at[slot], returned.at[seq], home_sems.at[0, slot], ahead(slot), tp
+                )
+
+    def mix_b(places):
+        span = pl.ds(places[0], len(places))
+        which = 0 if places[0] == 0 else 1
+        for slot in range(1, n_seq):
+            arrived(back_b.at[behind(slot), span], home_sems.at[1 + which, slot])
+        for place in places:
+            terms = back_b[:, place].reshape(n_seq * 8, width - split)
+            for c in range(2):
+                mixed_b[c, place] = mixture(place, c, terms).astype(BF16)
+
+    mix_b((0, 1, 2))
+    home(low_order[0])
+    home(high_order[0])
+    mix_b((3,))
+    copies.start(mixed_b.at[1 - core], mixed_pair, attn_sems.at[11], seq, partner)
+    arrived(mixed_pair, attn_sems.at[11])
+    for place in (3, 1, 2):
+        mixed_sum[place - 1] = (
+            mixed_b[core, place].astype(F32) + mixed_pair[place].astype(F32)
+        ).astype(BF16)
+        copies.start(
+            mixed_sum.at[place - 1],
+            mixed_in_b.at[place - 1],
+            attn_sems.at[11 + place],
+            seq,
+            peer(place, False),
+        )
+    for low, high in zip(low_order[1:], high_order[1:]):
+        home(low)
+        home(high)
     returned[seq] = final[0]
-    pickers = [split3(table[1]) for table in tables]
+    total_b = mixed_b[core, 0].astype(F32) + mixed_pair[0].astype(F32)
+    for place in (1, 2, 3):
+        arrived(mixed_in_b.at[place - 1], attn_sems.at[11 + place])
+        total_b = total_b + mixed_in_b[place - 1].astype(F32)
+    residual[:, split:] = residual[:, split:] + total_b
     for slot in range(1, n_seq):
-        arrived(returned.at[behind(slot)], home_sems.at[slot])
-    terms = returned[...].reshape(n_seq * 8, width)
+        arrived(returned.at[behind(slot)], home_sems.at[0, slot])
+    terms = returned[...].reshape(n_seq * 8, split)
     for c in range(2):
-        mixed[c] = sum(contract_first(piece, terms) for piece in pickers[c])
+        mixed[c] = mixture(0, c, terms)
     copies.start(mixed.at[1 - core], mixed_in, attn_sems.at[10], seq, partner)
+    out[:, split:] = residual[:, split:].astype(BF16)
     arrived(mixed_in, attn_sems.at[10])
-    out[...] = (residual[...] + (mixed[core] + mixed_in[...])).astype(BF16)
+    out[:, :split] = (residual[:, :split] + (mixed[core] + mixed_in[...])).astype(BF16)
     copies.drain()
 
 
@@ -474,6 +626,8 @@
     heads_width = w_out.shape[0]
     vmem, dma = pltpu.VMEM, pltpu.SemaphoreType.DMA
     chunks = n_seq // max(1, n_seq // 4)
+    split = width * 2 // 3 // 128 * 128
+    rest = width - split
     scratch = [
         vmem((width, length), BF16),
         vmem((width, columns), BF16),
@@ -481,37 +635,52 @@
         vmem((length, 128), BF16),
         vmem((length, 128), BF16),
         vmem((n_tp, count, width), BF16),
-        vmem((2, 2 * TOPK, count), F32),
+        vmem((n_tp, 2 * TOPK, count), F32),
         vmem((n_x, 2, 2, count // 2, width), BF16),
         vmem((n_x, 2, count // 2, width), BF16),
         vmem((n_x, 2, count // 2, width), BF16),
         vmem((2, count // 2, width), BF16),
         vmem((2, 2, count // 2, width), BF16),
         vmem((count, width), F32),
-        vmem((2, count, width), BF16),
-        vmem((n_seq, 8, width), BF16),
-        vmem((2, n_x, n_seq, 8, width), BF16),
+        vmem((2, count, split), BF16),
+        vmem((n_tp, count, rest), BF16),
+        vmem((n_seq, 8, split), BF16),
+        vmem((n_seq, n_x, 8, rest), BF16),
+        vmem((2, n_x, n_seq, 8, split), BF16),
+        vmem((2, n_seq, n_x, 8, rest), BF16),
         vmem((2, 2, hidden, width), BF16),
         vmem((2, hidden, width), BF16),
-        vmem((2, n_x, n_seq, 8, width), BF16),
-        vmem((n_x, n_seq, 8, width), BF16),
-        vmem((n_x, n_seq, 8, width), BF16),
-        vmem((n_seq, 8, width), BF16),
-        vmem((2, n_seq, 8, width), BF16),
-        vmem((n_seq, 8, width), BF16),
-        vmem((n_seq, 8, width), BF16),
-        vmem((2, count, width), F32),
-        vmem((count, width), F32),
+        vmem((2, 3, 2, n_seq * 8, hidden), F32),
+        vmem((2, n_x, n_seq, 8, split), BF16),
+        vmem((2, n_seq, n_x, 8, rest), BF16),
+        vmem((n_x, n_seq, 8, split), BF16),
+        vmem((n_seq, n_x, 8, rest), BF16),
+        vmem((n_x, n_seq, 8, split), BF16),
+        vmem((n_seq, n_x, 8, rest), BF16),
+        vmem((n_seq, 8, split), BF16),
+        vmem((2, n_seq, 8, split), BF16),
+        vmem((n_seq, 8, split), BF16),
+        vmem((n_seq, 8, split), BF16),
+        vmem((n_seq, n_x, 8, rest), BF16),
+        vmem((2, n_x, count, rest), BF16),
+        vmem((n_x, count, rest), BF16),
+        vmem((3, count, rest), BF16),
+        vmem((3, count, rest), BF16),
+        vmem((2, count, split), F32),
+        vmem((count, split), F32),
         dma((7,)),
-        dma((160,)),
-        dma((11,)),
-        dma((chunks,)),
+        dma((256,)),
+        dma((15,)),
+        dma((n_tp,)),
+        dma((n_tp,)),
+        dma((2, chunks)),
         dma((3, chunks)),
-        dma((4, chunks)),
+        dma((5, chunks)),
         dma((4, chunks)),
         dma((chunks,)),
         dma((2, chunks)),
-        dma((n_seq,)),
+        dma((3, n_seq)),
+        dma((4,)),
     ]
     in_vmem = pl.BlockSpec(memory_space=pltpu.VMEM)
     return pl.pallas_call(

time: 107 us -> 94.3 us (0.88)
  Pallas kernels: 105 us -> 92.6 us
    pallas_call x1, Pallas kernels: 105 us -> 92.6 us  [local(): pl.pallas_call(functools.partial(layer_kernel, n_seq, n_x), out_shape=jax...]
where the time goes in v4:
time: 94.3 us; the launch traced here: 94.1 us
  Pallas kernels  92.6 us (98%)
  local copies, waits for them, and re-layouts  1.54 us (2%)
    pallas_call x1, Pallas kernels, local(): pl.pallas_call(functools.partial(layer_kernel, n_seq, n_x), out_shape=jax...  92.6 us

profile of v4, /device:TPU:1, one launch (start us, length us, event | category | flops | bytes accessed | tf_op | source)
XLA Modules:
  0.0 94.1 jit_solution(14428596397666717564)
XLA Ops:
  0.0 92.6 %shard_map.100 = bf16[16,2880]{1,0:T(8,128)(2,1)} custom-call(s32[4,16]{1,0:T(4,128)} %bitcast.12, f32[4,16]{1,0:T(4,128)} %bitcast.13, f32[2880]{0:T(1024)} %attn_gain.1, f32[2880]{0:T(1024)} %mlp_gain.1, bf16[128,128]{1,0:T(8,128)(2,1)} %bitcast.11, bf16[2880,128]{1,0:T(8,128)(2,1)} %bitcast.10, bf16[2880,640]{1,0:T(8,128)(2,1)} %bitcast.8, ...), custom_call_target="tpu_custom_call" | custom-call | tf_op jit(solution)/shard_map/pallas_call | solution.py:686
  92.6 1.5 %copy.12 = bf16[16,2880]{1,0:T(8,128)(2,1)} copy(bf16[16,2880]{1,0:T(8,128)(2,1)} %shard_map.100) | data formatting | bytes 184320

commit v5 on v4

--- a/solution.py
+++ b/solution.py
@@ -98,10 +98,12 @@
     )
 
 
-def slot_table(route, core, n_seq, slot_core):
-    count = route.shape[1]
-    shape = (n_seq * 8, count)
+def slot_tables(routes, core, n_seq):
+    count = routes[0].shape[1]
+    route = jnp.concatenate(routes, axis=1)
+    shape = (n_seq * 8, route.shape[1])
     line = lax.broadcasted_iota(jnp.int32, shape, 0)
+    token = lax.broadcasted_iota(jnp.int32, shape, 1)
     expert = (line // 8 * 2 + core).astype(F32)
     chosen = jnp.zeros(shape, F32)
     weight = jnp.zeros(shape, F32)
@@ -109,12 +111,15 @@
         named = expert == route[k : k + 1, :]
         chosen = chosen + named.astype(F32)
         weight = weight + jnp.where(named, route[TOPK + k : TOPK + k + 1, :], 0.0)
-    before = lax.broadcasted_iota(jnp.int32, (count, count), 0) < lax.broadcasted_iota(
-        jnp.int32, (count, count), 1
+    square = (shape[1], shape[1])
+    one = lax.broadcasted_iota(jnp.int32, square, 0)
+    two = lax.broadcasted_iota(jnp.int32, square, 1)
+    before = (one < two) & (one // count == two // count)
+    rank = jnp.dot(
+        chosen.astype(BF16), before.astype(F32).astype(BF16), preferred_element_type=F32
     )
-    rank = jnp.dot(chosen.astype(BF16), before.astype(BF16), preferred_element_type=F32)
     place = (line % 4).astype(F32)
-    here = line % 8 // 4 == slot_core
+    here = line % 8 // 4 == token // count % 2
     hit = jnp.where(here & (rank == place), chosen, 0.0)
     return hit.astype(BF16), hit * weight
 
@@ -155,6 +160,7 @@
     residual,
     hidden_a,
     hidden_b,
+    pickers,
     packed_a,
     packed_b,
     rows,
@@ -278,10 +284,16 @@
     copies.start(part.at[:, 1 - core], attn_pair, attn_sems.at[2], seq, partner)
     for other in peers:
         arrived(route.at[other], route_sems.at[other])
-    tables = [
-        [slot_table(route[order[place] * 2 + c], core, n_seq, c) for c in range(2)]
-        for place in range(4)
-    ]
+    placer, weighted = slot_tables(
+        [route[order[place] * 2 + c] for place in range(4) for c in range(2)], core, n_seq
+    )
+    wide = 2 * out.shape[0]
+    placers = [placer[:, place * wide : (place + 1) * wide] for place in range(4)]
+    pieces = split3(weighted)
+    for place in range(4):
+        pickers[place] = jnp.concatenate(
+            [piece[:, place * wide : (place + 1) * wide] for piece in pieces], axis=1
+        )
     arrived(attn_pair, attn_sems.at[2])
 
     def pair_total(peer_x):
@@ -317,13 +329,13 @@
         copies.start(hidden_b.at[tp], hidden_b.at[tp], hidden_sems.at[tp], seq, other)
     arrived(hidden_a.at[1 - core], attn_sems.at[9])
 
-    def pack(place, first, second):
-        both = jnp.dot(tables[place][0][0], first, preferred_element_type=F32) + jnp.dot(
-            tables[place][1][0], second, preferred_element_type=F32
-        )
-        return both.reshape(n_seq, 8, -1).astype(BF16)
-
-    packed_a[...] = pack(0, hidden_a[0], hidden_a[1])
+    def pack(place, both):
+        taken = jnp.dot(
+            placers[place], both.reshape(wide, -1), preferred_element_type=F32
+        )
+        return taken.reshape(n_seq, 8, -1).astype(BF16)
+
+    packed_a[...] = pack(0, hidden_a[...])
     for group in first_order:
         for slot in range(group * chunk, (group + 1) * chunk):
             if slot:
@@ -335,9 +347,7 @@
     for other in peers:
         arrived(hidden_b.at[other], hidden_sems.at[other])
     for place in range(4):
-        packed_b[:, place] = pack(
-            place, hidden_b[order[place] * 2], hidden_b[order[place] * 2 + 1]
-        )
+        packed_b[:, place] = pack(place, hidden_b[pl.ds(order[place] * 2, 2)])
     for group in first_order:
         for slot in range(group * chunk, (group + 1) * chunk):
             if slot:
@@ -538,10 +548,10 @@
                 chip_sum.at[peer_x, at], ring_in.at[side, at], in_sems.at[side, group], seq, target
             )
 
-    pickers = [[split3(tables[place][c][1]) for c in range(2)] for place in range(4)]
-
-    def mixture(place, c, terms):
-        return sum(contract_first(piece, terms) for piece in pickers[place][c])
+    def mixture(place, terms):
+        parts = contract_first(pickers[place], terms)
+        whole = parts[:wide] + parts[wide : 2 * wide] + parts[2 * wide :]
+        return whole.reshape(2, wide // 2, -1)
 
     def home(group):
         at = slots(group)
@@ -563,14 +573,16 @@
             arrived(back_b.at[behind(slot), span], home_sems.at[1 + which, slot])
         for place in places:
             terms = back_b[:, place].reshape(n_seq * 8, width - split)
-            for c in range(2):
-                mixed_b[c, place] = mixture(place, c, terms).astype(BF16)
+            mixed_b[:, place] = mixture(place, terms).astype(BF16)
 
     mix_b((0, 1, 2))
     home(low_order[0])
     home(high_order[0])
     mix_b((3,))
     copies.start(mixed_b.at[1 - core], mixed_pair, attn_sems.at[11], seq, partner)
+    for low, high in zip(low_order[1:], high_order[1:]):
+        home(low)
+        home(high)
     arrived(mixed_pair, attn_sems.at[11])
     for place in (3, 1, 2):
         mixed_sum[place - 1] = (
@@ -583,9 +595,6 @@
             seq,
             peer(place, False),
         )
-    for low, high in zip(low_order[1:], high_order[1:]):
-        home(low)
-        home(high)
     returned[seq] = final[0]
     total_b = mixed_b[core, 0].astype(F32) + mixed_pair[0].astype(F32)
     for place in (1, 2, 3):
@@ -595,8 +604,7 @@
     for slot in range(1, n_seq):
         arrived(returned.at[behind(slot)], home_sems.at[0, slot])
     terms = returned[...].reshape(n_seq * 8, split)
-    for c in range(2):
-        mixed[c] = mixture(0, c, terms)
+    mixed[...] = mixture(0, terms)
     copies.start(mixed.at[1 - core], mixed_in, attn_sems.at[10], seq, partner)
     out[:, split:] = residual[:, split:].astype(BF16)
     arrived(mixed_in, attn_sems.at[10])
@@ -626,7 +634,7 @@
     heads_width = w_out.shape[0]
     vmem, dma = pltpu.VMEM, pltpu.SemaphoreType.DMA
     chunks = n_seq // max(1, n_seq // 4)
-    split = width * 2 // 3 // 128 * 128
+    split = width * 5 // 8 // 128 * 128
     rest = width - split
     scratch = [
         vmem((width, length), BF16),
@@ -644,6 +652,7 @@
         vmem((count, width), F32),
         vmem((2, count, split), BF16),
         vmem((n_tp, count, rest), BF16),
+        vmem((n_x, n_seq * 8, 6 * count), BF16),
         vmem((n_seq, 8, split), BF16),
         vmem((n_seq, n_x, 8, rest), BF16),
         vmem((2, n_x, n_seq, 8, split), BF16),

time: 94.3 us -> 91.7 us (0.972)
  Pallas kernels: 92.6 us -> 90 us
    pallas_call x1, Pallas kernels: 92.6 us -> 90 us  [local(): pl.pallas_call(functools.partial(layer_kernel, n_seq, n_x), out_shape=jax...]
where the time goes in v5:
time: 91.7 us; the launch traced here: 91.5 us
  Pallas kernels  90 us (98%)
  local copies, waits for them, and re-layouts  1.54 us (2%)
    pallas_call x1, Pallas kernels, local(): pl.pallas_call(functools.partial(layer_kernel, n_seq, n_x), out_shape=jax...  90 us

profile of v5, /device:TPU:1, one launch (start us, length us, event | category | flops | bytes accessed | tf_op | source)
XLA Modules:
  0.0 91.5 jit_solution(15761156067247112343)
XLA Ops:
  0.0 90.0 %shard_map.100 = bf16[16,2880]{1,0:T(8,128)(2,1)} custom-call(s32[4,16]{1,0:T(4,128)} %bitcast.12, f32[4,16]{1,0:T(4,128)} %bitcast.13, f32[2880]{0:T(1024)} %attn_gain.1, f32[2880]{0:T(1024)} %mlp_gain.1, bf16[128,128]{1,0:T(8,128)(2,1)} %bitcast.11, bf16[2880,128]{1,0:T(8,128)(2,1)} %bitcast.10, bf16[2880,640]{1,0:T(8,128)(2,1)} %bitcast.8, ...), custom_call_target="tpu_custom_call" | custom-call | tf_op jit(solution)/shard_map/pallas_call | solution.py:695
  90.0 1.5 %copy.12 = bf16[16,2880]{1,0:T(8,128)(2,1)} copy(bf16[16,2880]{1,0:T(8,128)(2,1)} %shard_map.100) | data formatting | bytes 184320

commit v6 on v5

--- a/solution.py
+++ b/solution.py
@@ -87,7 +87,7 @@
         before = contract_last(queries, keys[side]) * HEAD_SIZE ** (-0.5)
         scores = jnp.concatenate([jnp.where(later, before, -1e30), own[side]], axis=1)
         exponent = jnp.exp(scores - jnp.max(scores, axis=-1, keepdims=True))
-        weights = (exponent / jnp.sum(exponent, axis=-1, keepdims=True)).astype(BF16)
+        weights = (exponent * (1.0 / jnp.sum(exponent, axis=-1, keepdims=True))).astype(BF16)
         both = jnp.concatenate([values[side], own_values[side]], axis=0)
         term = jnp.dot(weights, both, preferred_element_type=F32)
         attended = term if attended is None else attended + term
@@ -392,60 +392,75 @@
         own = rows_b.at[core, slots(group)]
         copies.start(own, own, pair_sems.at[4, group], seq, partner)
 
-    def entered(place, expert, which):
-        taken = rows[expert, order[place]].reshape(n_seq * 8, split)
-        return contract_last(taken, w_gateup[expert, which, :, 0:split])
+    def taken_a(expert, places):
+        return jnp.concatenate(
+            [rows[expert, order[place]].reshape(n_seq * 8, split) for place in places], axis=0
+        )
+
+    def taken_b(expert, places):
+        return jnp.concatenate(
+            [rows_b[expert, :, place].reshape(n_seq * 8, width - split) for place in places], axis=0
+        )
 
     def enter(place):
         for group in range(chunks):
             arrived(rows.at[1 - core, order[place], slots(group)], pair_sems.at[place, group])
 
-    def early(place):
-        enter(place)
+    def early(places):
+        for place in places:
+            enter(place)
+        lines = pl.ds(places[0] * n_seq * 8, len(places) * n_seq * 8)
 
         def one(expert, carry):
+            taken = taken_a(expert, places)
             for which in range(2):
-                sums[expert, place, which] = entered(place, expert, which)
+                sums[expert, which, lines] = contract_last(
+                    taken, w_gateup[expert, which, :, 0:split]
+                )
             return carry
 
         lax.fori_loop(0, 2, one, 0)
 
-    def finish(place, expert, gate, up):
-        taken = rows_b[expert, :, place].reshape(n_seq * 8, width - split)
-        gate = gate + contract_last(taken, w_gateup[expert, 0, :, split:])
-        up = up + contract_last(taken, w_gateup[expert, 1, :, split:])
+    def finish(places, expert, ready):
+        taken = taken_b(expert, places)
+        gate = contract_last(taken, w_gateup[expert, 0, :, split:])
+        up = contract_last(taken, w_gateup[expert, 1, :, split:])
+        if ready:
+            gate, up = gate + sums[expert, 0], up + sums[expert, 1]
+        else:
+            taken = taken_a(expert, places)
+            gate = gate + contract_last(taken, w_gateup[expert, 0, :, 0:split])
+            up = up + contract_last(taken, w_gateup[expert, 1, :, 0:split])
         activated = (gate / (1.0 + jnp.exp(-gate)) * up).astype(BF16)
-        result = jnp.dot(activated, w_down[expert], preferred_element_type=F32)
-        result = result.reshape(n_seq, 8, width).astype(BF16)
-        product[expert, order[place]] = result[:, :, :split]
-        product_b[expert, :, place] = result[:, :, split:]
-
-    def block(place, ready):
-        def one(expert):
-            if ready:
-                gate, up = sums[expert, place, 0], sums[expert, place, 1]
-            else:
-                gate, up = entered(place, expert, 0), entered(place, expert, 1)
-            finish(place, expert, gate, up)
-
-        one(1 - core)
-        block_x = order[place]
-        for group in range(chunks):
+        for a, b, target in ((0, split, product), (split, width, product_b)):
+            result = jnp.dot(activated, w_down[expert, :, a:b], preferred_element_type=F32)
+            result = result.reshape(len(places), n_seq, 8, b - a).astype(BF16)
+            for at, place in enumerate(places):
+                if a == 0:
+                    target[expert, order[place]] = result[at]
+                else:
+                    target[expert, :, place] = result[at]
+
+    def block(places, ready):
+        finish(places, 1 - core, ready)
+        for place in places:
+            block_x = order[place]
+            for group in range(chunks):
+                copies.start(
+                    product.at[1 - core, block_x, slots(group)],
+                    from_pair.at[block_x, slots(group)],
+                    back_sems.at[place, group],
+                    seq,
+                    partner,
+                )
             copies.start(
-                product.at[1 - core, block_x, slots(group)],
-                from_pair.at[block_x, slots(group)],
-                back_sems.at[place, group],
+                product_b.at[1 - core, :, place],
+                from_pair_b.at[:, place],
+                mix_sems.at[place],
                 seq,
                 partner,
             )
-        copies.start(
-            product_b.at[1 - core, :, place],
-            from_pair_b.at[:, place],
-            mix_sems.at[place],
-            seq,
-            partner,
-        )
-        one(core)
+        finish(places, core, ready)
 
     def pair_sum_b(places):
         for place in places:
@@ -474,28 +489,30 @@
             product[core, block_x, at].astype(F32) + from_pair[block_x, at].astype(F32)
         ).astype(BF16)
 
-    for group in first_order[:-1]:
+    for group in first_order:
         spread(group)
     take(True, 0)
-    if half in first_order[:-1]:
-        take(False, half)
-    spread(first_order[-1])
+    take(False, half)
     take(False, chunks - 1)
     for copy in weight_loads:
         copy.wait()
-    early(0)
+    early((0,))
     for group in first_order:
         take(True, group)
         take(False, group)
     for group in first_order:
         take_b(group)
-    early(1)
-    early(2)
+    early((1, 2))
     for group in first_order:
         arrived(rows_b.at[1 - core, slots(group)], pair_sems.at[4, group])
-    block(0, True)
-    block(1, True)
-    block(2, True)
+    def take_far(group):
+        got = rows.at[core, far_x, slots(group)]
+        arrived(got, ring_sems.at[2, group])
+        copies.start(got, got, pair_sems.at[3, group], seq, partner)
+
+    for group in first_order[:-1]:
+        take_far(group)
+    block((0, 1, 2), True)
     for group in high_order:
         pair_sum(right_x, 2, group)
         copies.start(
@@ -514,14 +531,10 @@
             seq,
             left,
         )
-
-    for group in range(chunks):
-        got = rows.at[core, far_x, slots(group)]
-        arrived(got, ring_sems.at[2, group])
-        copies.start(got, got, pair_sems.at[3, group], seq, partner)
+    take_far(first_order[-1])
     pair_sum_b((0, 1, 2))
     enter(3)
-    block(3, False)
+    block((3,), False)
     for low, high in zip(low_order, high_order):
         pair_sum(far_x, 3, low)
         copies.start(
@@ -531,12 +544,12 @@
         copies.start(
             chip_sum.at[far_x, slots(high)], ring_opp.at[slots(high)], opp_sems.at[high], seq, left
         )
+    pair_sum_b((3,))
     for low, high in zip(low_order, high_order):
         pair_sum(right_x, 2, low)
         pair_sum(left_x, 1, high)
         pair_sum(x, 0, low)
         pair_sum(x, 0, high)
-    pair_sum_b((3,))
     for low, high in zip(low_order, high_order):
         for group, peer_x, target, side in ((low, right_x, right, 0), (high, left_x, left, 1)):
             at = slots(group)
@@ -659,7 +672,7 @@
         vmem((2, n_seq, n_x, 8, rest), BF16),
         vmem((2, 2, hidden, width), BF16),
         vmem((2, hidden, width), BF16),
-        vmem((2, 3, 2, n_seq * 8, hidden), F32),
+        vmem((2, 2, 3 * n_seq * 8, hidden), F32),
         vmem((2, n_x, n_seq, 8, split), BF16),
         vmem((2, n_seq, n_x, 8, rest), BF16),
         vmem((n_x, n_seq, 8, split), BF16),

time: 91.7 us -> 88.5 us (0.965)
  Pallas kernels: 90 us -> 86.8 us
    pallas_call x1, Pallas kernels: 90 us -> 86.8 us  [local(): pl.pallas_call(functools.partial(layer_kernel, n_seq, n_x), out_shape=jax...]
where the time goes in v6:
time: 88.5 us; the launch traced here: 88.3 us
  Pallas kernels  86.8 us (98%)
  local copies, waits for them, and re-layouts  1.54 us (2%)
    pallas_call x1, Pallas kernels, local(): pl.pallas_call(functools.partial(layer_kernel, n_seq, n_x), out_shape=jax...  86.8 us

profile of v6, /device:TPU:1, one launch (start us, length us, event | category | flops | bytes accessed | tf_op | source)
XLA Modules:
  0.0 88.3 jit_solution(6024255818962995892)
XLA Ops:
  0.0 86.8 %shard_map.100 = bf16[16,2880]{1,0:T(8,128)(2,1)} custom-call(s32[4,16]{1,0:T(4,128)} %bitcast.12, f32[4,16]{1,0:T(4,128)} %bitcast.13, f32[2880]{0:T(1024)} %attn_gain.1, f32[2880]{0:T(1024)} %mlp_gain.1, bf16[128,128]{1,0:T(8,128)(2,1)} %bitcast.11, bf16[2880,128]{1,0:T(8,128)(2,1)} %bitcast.10, bf16[2880,640]{1,0:T(8,128)(2,1)} %bitcast.8, ...), custom_call_target="tpu_custom_call" | custom-call | tf_op jit(solution)/shard_map/pallas_call | solution.py:708
  86.8 1.5 %copy.12 = bf16[16,2880]{1,0:T(8,128)(2,1)} copy(bf16[16,2880]{1,0:T(8,128)(2,1)} %shard_map.100) | data formatting | bytes 184320
